TPU v7x, 256 devices: a whole 4x4x8 slice. The times are simulated.
256 devices in a mesh: mom: 32 (over x, z), tm: 8 (over y, core).
Axes of the slice: x: 4, y: 4, z: 8, core: 2. Of those that a mesh axis runs over, the one named last changes fastest.
Arguments:
- source: float32 [2, 32, 2048, 512], P(None, 'mom', 'tm'), may hold values from -6 to 6
- inverse_diag: float32 [2, 32, 8, 256, 256], P(None, 'mom', 'tm'), may hold values from -0.25 to 0.25
- coupling: float32 [2, 32, 8, 256, 256], P(None, 'mom', 'tm'), may hold values from -0.21875 to 0.21875
- pair_moms: int32 [32, 8, 3], replicated, may hold values from 0 to 31, as said below
- pair_count: int32 [32], replicated, may hold values from 1 to 8
- pair_weight: int32 [32, 8], replicated, may hold values from 0 to 15
- vertex: float32 [16], replicated, may hold values from 0.02 to 0.2
Outputs:
- solved: bfloat16 [2, 32, 2048, 512], P(None, 'mom', 'tm')
- sigma: float32 [2, 32, 2048, 512], P(None, 'mom', 'tm')
Inputs may be any that keep to these rules, and one draw needn't show every extreme that they name: `pair_moms`: entry (k, s) is ((k - q) mod 32, p, (p + q) mod 32) for some q and p.
All inputs are finite; a program needn't handle non-finite values.
Results may differ from a plain program's by a relative error of at most 0.0059.
Values may be sent and summed in bfloat16 or wider, within the bound.
A program may use at most 64 MiB of HBM per device.

v0:
```python
import jax
import jax.numpy as jnp
from jax import lax
from jax.sharding import PartitionSpec as P


def from_behind(value, axis, steps):
    count = lax.axis_size(axis)
    leading, last = (max(0, -steps), min(count, count - steps))
    return lax.ppermute(value, axis, [(source, source + steps) for source in range(leading, last)])


def complex_mat(left, right):

    def real_mat(first, second):
        return jnp.einsum("kij,kjc->kic", first, second, precision=lax.Precision.HIGHEST)

    real_part = real_mat(left[0], right[0]) - real_mat(left[1], right[1])
    imag_part = real_mat(left[0], right[1]) + real_mat(left[1], right[0])
    return jnp.stack([real_part, imag_part])


def self_energy(greens, triples, live_count, weight_index, vertex):
    slots = triples.shape[1]
    entries = vertex.shape[0]
    table = jnp.sum(
        jnp.where(weight_index[..., None] == jnp.arange(entries, dtype=jnp.int32), vertex, 0.0), -1
    )
    live_mask = jnp.arange(slots, dtype=jnp.int32)[None, :] < live_count[:, None]
    scaled = jnp.where(live_mask, table, 0.0)
    total = jnp.zeros((2, triples.shape[0], greens.shape[2], greens.shape[3]), jnp.float32)
    for pair_slot in range(slots):
        first = jnp.take(greens, triples[:, pair_slot, 0], axis=1).astype(jnp.float32)
        second = jnp.take(greens, triples[:, pair_slot, 1], axis=1).astype(jnp.float32)
        third = jnp.take(greens, triples[:, pair_slot, 2], axis=1).astype(jnp.float32)
        prod_re = first[0] * second[0] - first[1] * second[1]
        prod_im = first[0] * second[1] + first[1] * second[0]
        term_re = prod_re * third[0] + prod_im * third[1]
        term_im = prod_im * third[0] - prod_re * third[1]
        factor = scaled[:, pair_slot][:, None, None]
        total = total + factor * jnp.stack([term_re, term_im])
    return total


def local(source, inverse_diag, coupling, pair_moms, pair_count, pair_weight, vertex):
    mom_local = source.shape[1]
    block_size = inverse_diag.shape[3]
    columns = source.shape[3]
    unit_eye = jnp.broadcast_to(
        jnp.eye(block_size, dtype=jnp.float32), (mom_local, block_size, block_size)
    )
    identity_map = jnp.stack([unit_eye, jnp.zeros_like(unit_eye)])
    zero_state = jnp.zeros((2, mom_local, block_size, columns), jnp.float32)
    partial_value = zero_state
    propagator = identity_map
    inverse = inverse_diag[:, :, 0]
    coupled = coupling[:, :, 0]
    partial_value = complex_mat(inverse, source + complex_mat(coupled, partial_value))
    propagator = complex_mat(inverse, complex_mat(coupled, propagator))

    def relay_step(turn_index, incoming):
        return from_behind(complex_mat(propagator, incoming) + partial_value, "tm", 1)

    entering = lax.fori_loop(0, lax.axis_size("tm") - 1, relay_step, zero_state)
    greens = partial_value + complex_mat(propagator, entering)
    solved = greens.astype(jnp.bfloat16)
    result = self_energy(
        lax.all_to_all(solved, "mom", split_axis=2, concat_axis=1, tiled=True),
        pair_moms,
        pair_count,
        pair_weight,
        vertex,
    )
    sigma = lax.all_to_all(result, "mom", split_axis=1, concat_axis=2, tiled=True)
    return (solved, sigma)


def solution(mesh):
    return jax.shard_map(
        local,
        mesh=mesh,
        in_specs=(
            P(None, "mom", "tm", None),
            P(None, "mom", "tm", None, None),
            P(None, "mom", "tm", None, None),
            P(),
            P(),
            P(),
            P(),
        ),
        out_specs=(P(None, "mom", "tm", None), P(None, "mom", "tm", None)),
        check_vma=False,
    )
```

profile of v0, /device:TPU:8, one launch (start us, length us, event | category | flops | bytes accessed | tf_op | source)
XLA Modules:
  0.0 271.7 jit_solution(10973466227574073716)
XLA Ops:
  0.6 1.3 fusion.53
  3.2 1.0 fusion.35
  4.2 1.0 fusion.34
  5.9 1.0 fusion.18
  6.9 1.0 fusion.19
  8.7 1.0 pad_maximum_fusion
  9.8 1.6 copy.69
  14.0 140.3 %while.10 = (s32[]{:T(128)}, f32[2,1,256,512]{3,2,1,0:T(8,128)S(1)}, f32[1,256,256]{2,1,0:T(8,128)S(1)}, f32[1,256,256]{2,1,0:T(8,128)S(1)}, f32[2,1,256,512]{3,2,1,0:T(8,128)S(1)}, /*index=5*/s32[]{:T(128)}) while((s32[]{:T(128)}, f32[2,1,256,512]{3,2,1,0:T(8,128)S(1)}, f32[1,256,256]{2,1,0:T(8,128)S(1)}, f32[1,256,256]{2,1,0:T(8,128)S(1)}, ...), condition=%wide.region_3.4_spmd, body=%wide.region_2.3_spmd.sunk | while | flops 1611399168 | bytes 13631597 | solution.py:64
  16.7 1.2 maximum_add_fusion.4
  17.9 1.9 collective-permute-start
  19.8 14.4 %collective-permute-done = f32[2,1,256,512]{3,2,1,0:T(8,128)S(1)} collective-permute-done((f32[2,1,256,512]{3,2,1,0:T(8,128)}, f32[2,1,256,512]{3,2,1,0:T(8,128)S(1)}, u32[]{:S(2)}, u32[]{:S(2)}) %collective-permute-start) | collective-permute-done | bytes 1048608 | tf_op jit(solution)/shard_map/while/body/eval_jaxpr/ppermute | solution.py:10
  36.7 1.2 maximum_add_fusion.4
  37.9 1.9 collective-permute-start
  39.8 14.4 %collective-permute-done = f32[2,1,256,512]{3,2,1,0:T(8,128)S(1)} collective-permute-done((f32[2,1,256,512]{3,2,1,0:T(8,128)}, f32[2,1,256,512]{3,2,1,0:T(8,128)S(1)}, u32[]{:S(2)}, u32[]{:S(2)}) %collective-permute-start) | collective-permute-done | bytes 1048608 | tf_op jit(solution)/shard_map/while/body/eval_jaxpr/ppermute | solution.py:10
  56.7 1.2 maximum_add_fusion.4
  57.9 1.9 collective-permute-start
  59.8 14.4 %collective-permute-done = f32[2,1,256,512]{3,2,1,0:T(8,128)S(1)} collective-permute-done((f32[2,1,256,512]{3,2,1,0:T(8,128)}, f32[2,1,256,512]{3,2,1,0:T(8,128)S(1)}, u32[]{:S(2)}, u32[]{:S(2)}) %collective-permute-start) | collective-permute-done | bytes 1048608 | tf_op jit(solution)/shard_map/while/body/eval_jaxpr/ppermute | solution.py:10
  76.7 1.2 maximum_add_fusion.4
  77.9 1.9 collective-permute-start
  79.8 14.4 %collective-permute-done = f32[2,1,256,512]{3,2,1,0:T(8,128)S(1)} collective-permute-done((f32[2,1,256,512]{3,2,1,0:T(8,128)}, f32[2,1,256,512]{3,2,1,0:T(8,128)S(1)}, u32[]{:S(2)}, u32[]{:S(2)}) %collective-permute-start) | collective-permute-done | bytes 1048608 | tf_op jit(solution)/shard_map/while/body/eval_jaxpr/ppermute | solution.py:10
  96.7 1.2 maximum_add_fusion.4
  97.9 1.9 collective-permute-start
  99.8 14.4 %collective-permute-done = f32[2,1,256,512]{3,2,1,0:T(8,128)S(1)} collective-permute-done((f32[2,1,256,512]{3,2,1,0:T(8,128)}, f32[2,1,256,512]{3,2,1,0:T(8,128)S(1)}, u32[]{:S(2)}, u32[]{:S(2)}) %collective-permute-start) | collective-permute-done | bytes 1048608 | tf_op jit(solution)/shard_map/while/body/eval_jaxpr/ppermute | solution.py:10
  116.8 1.2 maximum_add_fusion.4
  117.9 1.9 collective-permute-start
  119.9 14.4 %collective-permute-done = f32[2,1,256,512]{3,2,1,0:T(8,128)S(1)} collective-permute-done((f32[2,1,256,512]{3,2,1,0:T(8,128)}, f32[2,1,256,512]{3,2,1,0:T(8,128)S(1)}, u32[]{:S(2)}, u32[]{:S(2)}) %collective-permute-start) | collective-permute-done | bytes 1048608 | tf_op jit(solution)/shard_map/while/body/eval_jaxpr/ppermute | solution.py:10
  136.8 1.2 maximum_add_fusion.4
  138.0 1.9 collective-permute-start
  139.9 14.4 %collective-permute-done = f32[2,1,256,512]{3,2,1,0:T(8,128)S(1)} collective-permute-done((f32[2,1,256,512]{3,2,1,0:T(8,128)}, f32[2,1,256,512]{3,2,1,0:T(8,128)S(1)}, u32[]{:S(2)}, u32[]{:S(2)}) %collective-permute-start) | collective-permute-done | bytes 1048608 | tf_op jit(solution)/shard_map/while/body/eval_jaxpr/ppermute | solution.py:10
  154.3 2.0 fusion.32
  156.3 1.0 fusion.28
  157.3 1.0 fusion.17
  158.3 1.0 fusion.16
  159.5 1.2 copy.74
  160.7 11.7 %all-to-all-start = ((bf16[2,1,256,512]{3,0,1,2:T(2,128)(2,1)}), bf16[2,1,256,512]{3,0,1,2:T(2,128)(2,1)S(1)}, u32[]{:S(2)}, u32[]{:S(2)}) async-start(bf16[2,1,256,512]{3,0,1,2:T(2,128)(2,1)} %copy.74), calls=%async_computation | async-start | bytes 1048576 | tf_op jit(solution)/shard_map/all_to_all | solution.py:68
  174.2 14.8 %all-to-all-done = bf16[2,1,256,512]{3,0,1,2:T(2,128)(2,1)S(1)} async-done(((bf16[2,1,256,512]{3,0,1,2:T(2,128)(2,1)}), bf16[2,1,256,512]{3,0,1,2:T(2,128)(2,1)S(1)}, u32[]{:S(2)}, u32[]{:S(2)}) %all-to-all-start) | async-done | bytes 524320 | tf_op jit(solution)/shard_map/all_to_all | solution.py:68
  189.0 1.4 gather_fusion.20
  190.4 1.4 gather_fusion.21
  191.8 1.4 gather_fusion.22
  193.1 1.4 gather_fusion.23
  194.5 1.4 gather_fusion.18
  195.9 1.4 gather_fusion.19
  197.4 1.4 gather_fusion.16
  198.7 1.4 gather_fusion.17
  200.1 1.4 gather_fusion.14
  201.5 1.4 gather_fusion.15
  202.9 1.4 gather_fusion.12
  204.3 1.4 gather_fusion.13
  205.7 1.4 gather_fusion.10
  207.0 1.4 gather_fusion.11
  208.4 1.4 gather_fusion.8
  209.8 1.4 gather_fusion.9
  211.2 1.4 gather_fusion.6
  212.6 1.4 gather_fusion.7
  214.0 1.4 gather_fusion.4
  215.3 1.4 gather_fusion.5
  219.1 1.5 bitcast_convert_fusion.2
  224.4 0.8 copy-done.16
  233.0 0.9 copy-done.6
  235.8 1.6 fusion.27
  237.4 5.2 %all-to-all-start.1 = ((f32[2,32,8,512]{3,2,0,1:T(8,128)}), f32[2,32,8,512]{3,2,0,1:T(8,128)S(1)}, u32[]{:S(2)}, u32[]{:S(2)}) async-start(f32[2,32,8,512]{3,2,0,1:T(8,128)} %fusion.27), calls=%async_computation.1 | async-start | bytes 2097152 | tf_op jit(solution)/shard_map/all_to_all | solution.py:74
  242.6 1.0 copy.77
  243.6 27.1 %all-to-all-done.1 = f32[2,32,8,512]{3,2,0,1:T(8,128)S(1)} async-done(((f32[2,32,8,512]{3,2,0,1:T(8,128)}), f32[2,32,8,512]{3,2,0,1:T(8,128)S(1)}, u32[]{:S(2)}, u32[]{:S(2)}) %all-to-all-start.1) | async-done | bytes 1048608 | tf_op jit(solution)/shard_map/all_to_all | solution.py:74
  270.7 1.1 copy.85
  (160 shorter events, 40.1 us)
Async XLA Ops:
  0.6 1.5 copy-start.24
  2.1 1.0 copy-start
  4.2 1.0 copy-start.5
  7.9 0.8 copy-start.1
  13.1 0.7 copy-start.3
  17.9 16.3 %collective-permute-start = (f32[2,1,256,512]{3,2,1,0:T(8,128)}, f32[2,1,256,512]{3,2,1,0:T(8,128)S(1)}, u32[]{:S(2)}, u32[]{:S(2)}) collective-permute-start(f32[2,1,256,512]{3,2,1,0:T(8,128)} %maximum_add_fusion.4), channel_id=1, source_target_pairs={{0,1},{1,2},{2,3},{3,4},{4,5},{5,6},{6,7},{8,9},{9,10},{10,11},{11... | collective-permute-start | bytes 3145736 | tf_op jit(solution)/shard_map/while/body/eval_jaxpr/ppermute | solution.py:10
  37.9 16.3 %collective-permute-start = (f32[2,1,256,512]{3,2,1,0:T(8,128)}, f32[2,1,256,512]{3,2,1,0:T(8,128)S(1)}, u32[]{:S(2)}, u32[]{:S(2)}) collective-permute-start(f32[2,1,256,512]{3,2,1,0:T(8,128)} %maximum_add_fusion.4), channel_id=1, source_target_pairs={{0,1},{1,2},{2,3},{3,4},{4,5},{5,6},{6,7},{8,9},{9,10},{10,11},{11... | collective-permute-start | bytes 3145736 | tf_op jit(solution)/shard_map/while/body/eval_jaxpr/ppermute | solution.py:10
  57.9 16.3 %collective-permute-start = (f32[2,1,256,512]{3,2,1,0:T(8,128)}, f32[2,1,256,512]{3,2,1,0:T(8,128)S(1)}, u32[]{:S(2)}, u32[]{:S(2)}) collective-permute-start(f32[2,1,256,512]{3,2,1,0:T(8,128)} %maximum_add_fusion.4), channel_id=1, source_target_pairs={{0,1},{1,2},{2,3},{3,4},{4,5},{5,6},{6,7},{8,9},{9,10},{10,11},{11... | collective-permute-start | bytes 3145736 | tf_op jit(solution)/shard_map/while/body/eval_jaxpr/ppermute | solution.py:10
  77.9 16.3 %collective-permute-start = (f32[2,1,256,512]{3,2,1,0:T(8,128)}, f32[2,1,256,512]{3,2,1,0:T(8,128)S(1)}, u32[]{:S(2)}, u32[]{:S(2)}) collective-permute-start(f32[2,1,256,512]{3,2,1,0:T(8,128)} %maximum_add_fusion.4), channel_id=1, source_target_pairs={{0,1},{1,2},{2,3},{3,4},{4,5},{5,6},{6,7},{8,9},{9,10},{10,11},{11... | collective-permute-start | bytes 3145736 | tf_op jit(solution)/shard_map/while/body/eval_jaxpr/ppermute | solution.py:10
  97.9 16.3 %collective-permute-start = (f32[2,1,256,512]{3,2,1,0:T(8,128)}, f32[2,1,256,512]{3,2,1,0:T(8,128)S(1)}, u32[]{:S(2)}, u32[]{:S(2)}) collective-permute-start(f32[2,1,256,512]{3,2,1,0:T(8,128)} %maximum_add_fusion.4), channel_id=1, source_target_pairs={{0,1},{1,2},{2,3},{3,4},{4,5},{5,6},{6,7},{8,9},{9,10},{10,11},{11... | collective-permute-start | bytes 3145736 | tf_op jit(solution)/shard_map/while/body/eval_jaxpr/ppermute | solution.py:10
  117.9 16.3 %collective-permute-start = (f32[2,1,256,512]{3,2,1,0:T(8,128)}, f32[2,1,256,512]{3,2,1,0:T(8,128)S(1)}, u32[]{:S(2)}, u32[]{:S(2)}) collective-permute-start(f32[2,1,256,512]{3,2,1,0:T(8,128)} %maximum_add_fusion.4), channel_id=1, source_target_pairs={{0,1},{1,2},{2,3},{3,4},{4,5},{5,6},{6,7},{8,9},{9,10},{10,11},{11... | collective-permute-start | bytes 3145736 | tf_op jit(solution)/shard_map/while/body/eval_jaxpr/ppermute | solution.py:10
  138.0 16.3 %collective-permute-start = (f32[2,1,256,512]{3,2,1,0:T(8,128)}, f32[2,1,256,512]{3,2,1,0:T(8,128)S(1)}, u32[]{:S(2)}, u32[]{:S(2)}) collective-permute-start(f32[2,1,256,512]{3,2,1,0:T(8,128)} %maximum_add_fusion.4), channel_id=1, source_target_pairs={{0,1},{1,2},{2,3},{3,4},{4,5},{5,6},{6,7},{8,9},{9,10},{10,11},{11... | collective-permute-start | bytes 3145736 | tf_op jit(solution)/shard_map/while/body/eval_jaxpr/ppermute | solution.py:10
  154.3 2.0 copy-start.4
  158.3 1.0 copy-start.2
  160.7 11.7 %copy-start.25 = (s32[32,8,3]{0,1,2:T(8,128)S(1)}, s32[32,8,3]{0,1,2:T(8,128)}, u32[]{:S(2)}) copy-start(s32[32,8,3]{0,1,2:T(8,128)} %param.14) | copy-start | bytes 9220
  160.7 28.2 %all-to-all-start = ((bf16[2,1,256,512]{3,0,1,2:T(2,128)(2,1)}), bf16[2,1,256,512]{3,0,1,2:T(2,128)(2,1)S(1)}, u32[]{:S(2)}, u32[]{:S(2)}) async-start(bf16[2,1,256,512]{3,0,1,2:T(2,128)(2,1)} %copy.74), calls=%async_computation | async-start | bytes 1048576 | tf_op jit(solution)/shard_map/all_to_all | solution.py:68
  172.8 0.7 copy-start.26
  172.8 0.7 copy-start.27
  173.5 0.7 copy-start.28
  219.1 1.5 copy-start.22
  219.1 1.5 copy-start.23
  221.2 1.0 copy-start.20
  221.2 1.2 copy-start.21
  223.0 1.0 copy-start.18
  223.0 1.2 copy-start.19
  224.2 1.0 copy-start.16
  224.2 1.2 copy-start.17
  226.0 1.0 copy-start.14
  226.0 1.2 copy-start.15
  227.8 1.0 copy-start.12
  227.8 1.2 copy-start.13
  229.0 1.0 copy-start.10
  229.0 1.2 copy-start.11
  230.8 1.0 copy-start.8
  230.8 1.2 copy-start.9
  232.8 1.0 copy-start.6
  232.8 1.2 copy-start.7
  237.4 33.2 %all-to-all-start.1 = ((f32[2,32,8,512]{3,2,0,1:T(8,128)}), f32[2,32,8,512]{3,2,0,1:T(8,128)S(1)}, u32[]{:S(2)}, u32[]{:S(2)}) async-start(f32[2,32,8,512]{3,2,0,1:T(8,128)} %fusion.27), calls=%async_computation.1 | async-start | bytes 2097152 | tf_op jit(solution)/shard_map/all_to_all | solution.py:74
where the time goes:
time: 273 us; the launch traced here: 272 us
  waiting for transfers between devices  143 us (52%)
  local copies, waits for them, and re-layouts  46.7 us (17%)
  starting transfers between devices  30.2 us (11%)
  matrix products  28.8 us (11%)
  other arithmetic  21.5 us (8%)
    ppermute x7, waiting for transfers between devices, from_behind(): lax.ppermute(value, axis, [(source, source + steps) for source in range(l...  101 us
    dot_general x42, matrix products, real_mat(): jnp.einsum('kij,kjc->kic', first, second, precision=lax.Precision.HIGHEST)  28.8 us
    all_to_all x1, waiting for transfers between devices, local(): lax.all_to_all(result, 'mom', split_axis=1, concat_axis=2, tiled=True)  27.1 us
    all_to_all x1, waiting for transfers between devices, local(): lax.all_to_all(solved, 'mom', split_axis=2, concat_axis=1, tiled=True)  14.8 us
    ppermute x7, starting transfers between devices, from_behind(): lax.ppermute(value, axis, [(source, source + steps) for source in range(l...  13.4 us
    unnamed x59, local copies, waits for them, and re-layouts  12.2 us
    all_to_all x1, starting transfers between devices, local(): lax.all_to_all(solved, 'mom', split_axis=2, concat_axis=1, tiled=True)  11.7 us
    gather x8, local copies, waits for them, and re-layouts, self_energy(): jnp.take(greens, triples[:, pair_slot, 1], axis=1).astype(jnp.float32)  10.3 us
  transfers between devices with their start and end apart: 9, of which 9 were waited for; matrix products, arithmetic and copies ran while one was open for 0% of the time, Pallas kernels for 0%

commit v1 on v0

v1 whole, which is shorter than its diff:
```python
import jax
import jax.numpy as jnp
from jax import lax
from jax.experimental import pallas as pl
from jax.experimental.pallas import tpu as pltpu
from jax.sharding import PartitionSpec as P

MESH = pl.DeviceIdType.MESH
LANES = 128


def split(value):
    high = value.astype(jnp.bfloat16)
    return high, (value - high.astype(jnp.float32)).astype(jnp.bfloat16)


def dot(left, right):
    return jnp.dot(left, right, preferred_element_type=jnp.float32)


def complex_times(high, low, value):
    rows, width = high.shape[1], value.shape[1] // 2
    value_high, value_low = split(value)
    both = dot(high, value_high) + (dot(high, value_low) + dot(low, value_high))
    real = both[:rows, :width] - both[rows:, width:]
    imag = both[:rows, width:] + both[rows:, :width]
    return real, imag


def kernel(
    moms, counts, weights, vertex, source_hbm, inverse_hbm, coupling_hbm,
    solved, sigma,
    source, inverse, coupling, left_high, left_low, step_high, step_low, driven, entering, greens,
    outbox, inbox, wide, formed, returned,
    load_sem, hop_send, hop_recv, in_send, in_recv, out_send, out_recv,
):
    n_mom, n_tm = lax.axis_size("mom"), lax.axis_size("tm")
    me, turn = lax.axis_index("mom"), lax.axis_index("tm")
    rows, chunks = driven.shape[1], driven.shape[0]
    share = rows // n_mom
    slots = moms.shape[1]

    loads = [
        pltpu.make_async_copy(inverse_hbm.at[:, 0, 0], inverse, load_sem.at[0]),
        pltpu.make_async_copy(coupling_hbm.at[:, 0, 0], coupling, load_sem.at[1]),
        pltpu.make_async_copy(source_hbm.at[:, 0], source, load_sem.at[2]),
    ]
    for load in loads:
        load.start()

    barrier = pltpu.get_barrier_semaphore()

    def greet(step, carry):
        other = lax.rem(me + step, n_mom)
        pl.semaphore_signal(barrier, inc=1, device_id={"mom": other, "tm": turn}, device_id_type=MESH)
        return carry

    lax.fori_loop(1, n_mom, greet, 0)

    for other in (lax.rem(turn + 1, n_tm), lax.rem(turn + n_tm - 1, n_tm)):
        pl.semaphore_signal(barrier, inc=1, device_id={"mom": me, "tm": other}, device_id_type=MESH)

    for load in loads:
        load.wait()

    for part in range(2):
        high, low = split(inverse[part])
        left_high[part * rows:(part + 1) * rows, :] = high
        left_low[part * rows:(part + 1) * rows, :] = low
    step = complex_times(
        left_high[...], left_low[...], jnp.concatenate([coupling[0], coupling[1]], axis=1)
    )
    for part in range(2):
        high, low = split(step[part])
        step_high[part * rows:(part + 1) * rows, :] = high
        step_low[part * rows:(part + 1) * rows, :] = low

    def drive(chunk, carry):
        columns = pl.ds(pl.multiple_of(chunk * LANES, LANES), LANES)
        forcing = jnp.concatenate([source[0, :, columns], source[1, :, columns]], axis=1)
        real, imag = complex_times(left_high[...], left_low[...], forcing)
        driven[chunk] = jnp.concatenate([real, imag], axis=1)
        return carry

    lax.fori_loop(0, chunks, drive, 0)

    pl.semaphore_wait(barrier, n_mom + 1)

    def hop(chunk):
        return pltpu.make_async_remote_copy(
            src_ref=greens.at[chunk], dst_ref=entering.at[chunk],
            send_sem=hop_send.at[chunk], recv_sem=hop_recv.at[chunk],
            device_id={"mom": me, "tm": lax.rem(turn + 1, n_tm)}, device_id_type=MESH,
        )

    def scatter(chunk, other):
        return pltpu.make_async_remote_copy(
            src_ref=outbox.at[chunk, other], dst_ref=inbox.at[chunk, me],
            send_sem=in_send.at[chunk], recv_sem=in_recv.at[chunk],
            device_id={"mom": other, "tm": turn}, device_id_type=MESH,
        )

    def collect(chunk, other):
        return pltpu.make_async_remote_copy(
            src_ref=formed.at[chunk, other], dst_ref=returned.at[chunk, me],
            send_sem=out_send.at[chunk], recv_sem=out_recv.at[chunk],
            device_id={"mom": other, "tm": turn}, device_id_type=MESH,
        )

    def settle(buffer, chunk, sem):
        block = buffer.at[chunk, pl.ds(0, n_mom - 1)]
        pltpu.make_async_copy(block, block, sem.at[chunk]).wait()

    def advance(chunk):
        @pl.when(turn == 0)
        def _():
            greens[chunk] = driven[chunk]

        @pl.when(turn > 0)
        def _():
            hop(chunk).wait_recv()
            real, imag = complex_times(step_high[...], step_low[...], entering[chunk])
            greens[chunk] = driven[chunk] + jnp.concatenate([real, imag], axis=1)

        @pl.when(turn < n_tm - 1)
        def _():
            hop(chunk).start()

        value = greens[chunk]
        real, imag = value[:, :LANES], value[:, LANES:]
        packed = jnp.concatenate(
            [real.reshape(n_mom, share, LANES), imag.reshape(n_mom, share, LANES)], axis=1
        )
        outbox[chunk] = packed.astype(jnp.bfloat16)
        inbox[chunk, me] = outbox[chunk, me]

        def send(step, carry):
            scatter(chunk, lax.rem(me + step, n_mom)).start()
            return carry

        lax.fori_loop(1, n_mom, send, 0)
        columns = pl.ds(pl.multiple_of(chunk * LANES, LANES), LANES)
        solved[0, 0, :, columns] = real.astype(jnp.bfloat16)
        solved[1, 0, :, columns] = imag.astype(jnp.bfloat16)

    def form(chunk):
        settle(inbox, chunk, in_recv)
        wide[...] = inbox[chunk].astype(jnp.float32)

        def one(step, carry):
            mom = lax.rem(me + step, n_mom)
            live = counts[mom]
            total_real = jnp.zeros((share, LANES), jnp.float32)
            total_imag = jnp.zeros((share, LANES), jnp.float32)
            for slot in range(slots):
                first, second, third = (wide[moms[place, slot, mom]] for place in range(3))
                factor = jnp.where(slot < live, vertex[weights[slot, mom]], 0.0)
                ar, ai = first[:share], first[share:]
                br, bi = second[:share], second[share:]
                cr, ci = third[:share], third[share:]
                prod_real = ar * br - ai * bi
                prod_imag = ar * bi + ai * br
                total_real = total_real + factor * (prod_real * cr + prod_imag * ci)
                total_imag = total_imag + factor * (prod_imag * cr - prod_real * ci)
            formed[chunk, mom] = jnp.concatenate([total_real, total_imag], axis=0).astype(jnp.bfloat16)

            @pl.when(step < n_mom)
            def _():
                collect(chunk, mom).start()

            return carry

        lax.fori_loop(1, n_mom + 1, one, 0)
        returned[chunk, me] = formed[chunk, me]

    def finish(chunk):
        settle(returned, chunk, out_recv)
        value = returned[chunk].astype(jnp.float32)
        columns = pl.ds(pl.multiple_of(chunk * LANES, LANES), LANES)
        sigma[0, 0, :, columns] = value[:, :share].reshape(rows, LANES)
        sigma[1, 0, :, columns] = value[:, share:].reshape(rows, LANES)

    def stage(step, carry):
        @pl.when(step < chunks)
        def _():
            advance(step)

        @pl.when((step >= 1) & (step < chunks + 1))
        def _():
            form(step - 1)

        @pl.when(step >= 2)
        def _():
            finish(step - 2)

        return carry

    lax.fori_loop(0, chunks + 2, stage, 0)

    def close(chunk, carry):
        @pl.when(turn < n_tm - 1)
        def _():
            hop(chunk).wait_send()

        settle(outbox, chunk, in_send)
        settle(formed, chunk, out_send)
        return carry

    lax.fori_loop(0, chunks, close, 0)


def local(source, inverse_diag, coupling, pair_moms, pair_count, pair_weight, vertex):
    rows, columns = source.shape[2], source.shape[3]
    n_mom = lax.axis_size("mom")
    chunks, share = columns // LANES, rows // n_mom
    f32, bf16 = jnp.float32, jnp.bfloat16
    smem = pl.BlockSpec(memory_space=pltpu.SMEM)
    vmem = pl.BlockSpec(memory_space=pltpu.VMEM)
    hbm = pl.BlockSpec(memory_space=pl.ANY)
    piece = (chunks, n_mom, 2 * share, LANES)
    sems = pltpu.SemaphoreType.DMA((chunks,))
    return pl.pallas_call(
        kernel,
        out_shape=(
            jax.ShapeDtypeStruct(source.shape, bf16),
            jax.ShapeDtypeStruct(source.shape, f32),
        ),
        in_specs=[smem] * 4 + [hbm] * 3,
        out_specs=(vmem, vmem),
        scratch_shapes=[
            pltpu.VMEM((2, rows, columns), f32),
            pltpu.VMEM((2, rows, rows), f32),
            pltpu.VMEM((2, rows, rows), f32),
            pltpu.VMEM((2 * rows, rows), bf16),
            pltpu.VMEM((2 * rows, rows), bf16),
            pltpu.VMEM((2 * rows, rows), bf16),
            pltpu.VMEM((2 * rows, rows), bf16),
            pltpu.VMEM((chunks, rows, 2 * LANES), f32),
            pltpu.VMEM((chunks, rows, 2 * LANES), f32),
            pltpu.VMEM((chunks, rows, 2 * LANES), f32),
            pltpu.VMEM(piece, bf16),
            pltpu.VMEM(piece, bf16),
            pltpu.VMEM(piece[1:], f32),
            pltpu.VMEM(piece, bf16),
            pltpu.VMEM(piece, bf16),
            pltpu.SemaphoreType.DMA((3,)),
            sems, sems, sems, sems, sems, sems,
        ],
        compiler_params=pltpu.CompilerParams(
            collective_id=0, has_side_effects=True, vmem_limit_bytes=32 << 20
        ),
    )(
        jnp.transpose(pair_moms, (2, 1, 0)), pair_count, jnp.transpose(pair_weight, (1, 0)), vertex,
        source, inverse_diag, coupling,
    )


def solution(mesh):
    return jax.shard_map(
        local,
        mesh=mesh,
        in_specs=(
            P(None, "mom", "tm", None),
            P(None, "mom", "tm", None, None),
            P(None, "mom", "tm", None, None),
            P(),
            P(),
            P(),
            P(),
        ),
        out_specs=(P(None, "mom", "tm", None), P(None, "mom", "tm", None)),
        check_vma=False,
    )
```

time: 273 us -> 68.6 us (0.25)
  the two profiles are of different devices: /device:TPU:8 before, /device:TPU:25 now
where the time goes in v1:
time: 68.6 us; the launch traced here: 68.3 us
  Pallas kernels  60.5 us (88%)
  local copies, waits for them, and re-layouts  7.12 us (10%)
    pallas_call x1, Pallas kernels, local(): pl.pallas_call(kernel, out_shape=(jax.ShapeDtypeStruct(source.shape, bf16...  60.5 us
    unnamed x16, local copies, waits for them, and re-layouts  7.12 us

profile of v1, /device:TPU:25, one launch (start us, length us, event | category | flops | bytes accessed | tf_op | source)
XLA Modules:
  0.0 68.3 jit_solution(9935952334788355692)
XLA Ops:
  0.6 0.0 copy-start.5
  0.6 0.0 copy-start.6
  0.7 0.6 copy-done.5
  1.3 0.0 copy-done.6
  1.3 0.0 copy-start
  1.3 1.2 %copy-done = f32[2,1,256,512]{3,2,1,0:T(8,128)S(1)} copy-done((f32[2,1,256,512]{3,2,1,0:T(8,128)S(1)}, f32[2,1,256,512]{3,2,1,0:T(8,128)}, u32[]{:S(2)}) %copy-start) | copy-done | bytes 1048600
  2.5 0.0 copy-start.1
  2.5 1.0 %copy-done.1 = f32[2,1,1,256,256]{4,3,2,1,0:T(8,128)S(1)} copy-done((f32[2,1,1,256,256]{4,3,2,1,0:T(8,128)S(1)}, f32[2,1,1,256,256]{4,3,2,1,0:T(8,128)}, u32[]{:S(2)}) %copy-start.1) | copy-done | bytes 524312
  3.6 0.0 copy-start.2
  3.6 1.0 %copy-done.2 = f32[2,1,1,256,256]{4,3,2,1,0:T(8,128)S(1)} copy-done((f32[2,1,1,256,256]{4,3,2,1,0:T(8,128)S(1)}, f32[2,1,1,256,256]{4,3,2,1,0:T(8,128)}, u32[]{:S(2)}) %copy-start.2) | copy-done | bytes 524312
  4.6 0.0 copy-start.3
  4.6 0.7 %copy-done.3 = s32[32,8,3]{0,1,2:T(8,128)S(1)} copy-done((s32[32,8,3]{0,1,2:T(8,128)S(1)}, s32[32,8,3]{0,1,2:T(8,128)}, u32[]{:S(2)}) %copy-start.3) | copy-done | bytes 3096
  5.3 0.0 copy-start.4
  5.3 0.7 %copy-done.4 = s32[32,8]{0,1:T(8,128)S(1)} copy-done((s32[32,8]{0,1:T(8,128)S(1)}, s32[32,8]{0,1:T(8,128)}, u32[]{:S(2)}) %copy-start.4) | copy-done | bytes 1048
  6.0 60.5 %shard_map.86 = (bf16[2,1,256,512]{3,2,1,0:T(8,128)(2,1)S(1)}, f32[2,1,256,512]{3,2,1,0:T(8,128)S(1)}) custom-call(s32[3,8,32]{2,1,0:T(8,128)S(1)} %bitcast.2, s32[32]{0:T(128)S(1)} %copy-done.5, s32[8,32]{1,0:T(8,128)S(1)} %bitcast.3, f32[16]{0:T(128)S(1)} %copy-done.6, f32[2,1,256,512]{3,2,1,0:T(8,128)S(1)} %copy-done, ...), custom_call_target="tpu_custom_call" | custom-call | tf_op jit(solution)/shard_map/pallas_call | solution.py:222
  66.5 0.8 %copy.11 = bf16[2,1,256,512]{3,2,1,0:T(8,128)(2,1)} copy(bf16[2,1,256,512]{3,2,1,0:T(8,128)(2,1)S(1)} %get-tuple-element.4) | data formatting | bytes 1048576
  67.3 1.0 %copy.12 = f32[2,1,256,512]{3,2,1,0:T(8,128)} copy(f32[2,1,256,512]{3,2,1,0:T(8,128)S(1)} %get-tuple-element.5) | data formatting | bytes 2097152
Async XLA Ops:
  0.6 0.7 copy-start.5
  0.6 0.7 copy-start.6
  1.3 1.2 %copy-start = (f32[2,1,256,512]{3,2,1,0:T(8,128)S(1)}, f32[2,1,256,512]{3,2,1,0:T(8,128)}, u32[]{:S(2)}) copy-start(f32[2,1,256,512]{3,2,1,0:T(8,128)} %source_hbm.1) | copy-start | bytes 3145732
  2.5 1.0 %copy-start.1 = (f32[2,1,1,256,256]{4,3,2,1,0:T(8,128)S(1)}, f32[2,1,1,256,256]{4,3,2,1,0:T(8,128)}, u32[]{:S(2)}) copy-start(f32[2,1,1,256,256]{4,3,2,1,0:T(8,128)} %inverse_hbm.1) | copy-start | bytes 1572868
  3.6 1.0 %copy-start.2 = (f32[2,1,1,256,256]{4,3,2,1,0:T(8,128)S(1)}, f32[2,1,1,256,256]{4,3,2,1,0:T(8,128)}, u32[]{:S(2)}) copy-start(f32[2,1,1,256,256]{4,3,2,1,0:T(8,128)} %coupling_hbm.1) | copy-start | bytes 1572868
  4.6 0.7 %copy-start.3 = (s32[32,8,3]{0,1,2:T(8,128)S(1)}, s32[32,8,3]{0,1,2:T(8,128)}, u32[]{:S(2)}) copy-start(s32[32,8,3]{0,1,2:T(8,128)} %param.10) | copy-start | bytes 9220
  5.3 0.7 %copy-start.4 = (s32[32,8]{0,1:T(8,128)S(1)}, s32[32,8]{0,1:T(8,128)}, u32[]{:S(2)}) copy-start(s32[32,8]{0,1:T(8,128)} %param.12) | copy-start | bytes 3076

commit v2 on v1

--- a/solution.py
+++ b/solution.py
@@ -28,11 +28,11 @@
 
 
 def kernel(
-    moms, counts, weights, vertex, source_hbm, inverse_hbm, coupling_hbm,
-    solved, sigma,
-    source, inverse, coupling, left_high, left_low, step_high, step_low, driven, entering, greens,
-    outbox, inbox, wide, formed, returned,
-    load_sem, hop_send, hop_recv, in_send, in_recv, out_send, out_recv,
+    moms_hbm, counts_hbm, weights_hbm, vertex_hbm, source_hbm, inverse_hbm, coupling_hbm,
+    solved_hbm, sigma_hbm,
+    moms, counts, weights, vertex, source, inverse, coupling, left_high, left_low, step_high, step_low, driven, entering, greens,
+    outbox, inbox, wide, formed, returned, solved, sigma,
+    load_sem, store_sem, hop_send, hop_recv, in_send, in_recv, out_send, out_recv,
 ):
     n_mom, n_tm = lax.axis_size("mom"), lax.axis_size("tm")
     me, turn = lax.axis_index("mom"), lax.axis_index("tm")
@@ -41,9 +41,16 @@
     slots = moms.shape[1]
 
     loads = [
-        pltpu.make_async_copy(inverse_hbm.at[:, 0, 0], inverse, load_sem.at[0]),
-        pltpu.make_async_copy(coupling_hbm.at[:, 0, 0], coupling, load_sem.at[1]),
-        pltpu.make_async_copy(source_hbm.at[:, 0], source, load_sem.at[2]),
+        pltpu.make_async_copy(here, there, load_sem.at[place])
+        for place, (here, there) in enumerate((
+            (inverse_hbm.at[:, 0, 0], inverse),
+            (source_hbm.at[:, 0], source),
+            (coupling_hbm.at[:, 0, 0], coupling),
+            (moms_hbm, moms),
+            (counts_hbm, counts),
+            (weights_hbm, weights),
+            (vertex_hbm, vertex),
+        ))
     ]
     for load in loads:
         load.start()
@@ -60,30 +67,33 @@
     for other in (lax.rem(turn + 1, n_tm), lax.rem(turn + n_tm - 1, n_tm)):
         pl.semaphore_signal(barrier, inc=1, device_id={"mom": me, "tm": other}, device_id_type=MESH)
 
-    for load in loads:
-        load.wait()
-
+    def drive(chunk):
+        columns = pl.ds(pl.multiple_of(chunk * LANES, LANES), LANES)
+        forcing = jnp.concatenate([source[0, :, columns], source[1, :, columns]], axis=1)
+        real, imag = complex_times(left_high[...], left_low[...], forcing)
+        driven[chunk] = jnp.concatenate([real, imag], axis=1)
+
+    loads[0].wait()
     for part in range(2):
         high, low = split(inverse[part])
         left_high[part * rows:(part + 1) * rows, :] = high
         left_low[part * rows:(part + 1) * rows, :] = low
-    step = complex_times(
-        left_high[...], left_low[...], jnp.concatenate([coupling[0], coupling[1]], axis=1)
-    )
-    for part in range(2):
-        high, low = split(step[part])
-        step_high[part * rows:(part + 1) * rows, :] = high
-        step_low[part * rows:(part + 1) * rows, :] = low
-
-    def drive(chunk, carry):
-        columns = pl.ds(pl.multiple_of(chunk * LANES, LANES), LANES)
-        forcing = jnp.concatenate([source[0, :, columns], source[1, :, columns]], axis=1)
-        real, imag = complex_times(left_high[...], left_low[...], forcing)
-        driven[chunk] = jnp.concatenate([real, imag], axis=1)
-        return carry
-
-    lax.fori_loop(0, chunks, drive, 0)
-
+    loads[1].wait()
+    drive(0)
+    loads[2].wait()
+
+    @pl.when(turn > 0)
+    def _():
+        step = complex_times(
+            left_high[...], left_low[...], jnp.concatenate([coupling[0], coupling[1]], axis=1)
+        )
+        for part in range(2):
+            high, low = split(step[part])
+            step_high[part * rows:(part + 1) * rows, :] = high
+            step_low[part * rows:(part + 1) * rows, :] = low
+
+    for load in loads[3:]:
+        load.wait()
     pl.semaphore_wait(barrier, n_mom + 1)
 
     def hop(chunk):
@@ -111,7 +121,16 @@
         block = buffer.at[chunk, pl.ds(0, n_mom - 1)]
         pltpu.make_async_copy(block, block, sem.at[chunk]).wait()
 
+    def store(which, chunk):
+        here, there = ((solved, solved_hbm), (sigma, sigma_hbm))[which]
+        columns = pl.ds(pl.multiple_of(chunk * LANES, LANES), LANES)
+        return pltpu.make_async_copy(here.at[chunk], there.at[:, 0, :, columns], store_sem.at[which, chunk])
+
     def advance(chunk):
+        @pl.when(chunk > 0)
+        def _():
+            drive(chunk)
+
         @pl.when(turn == 0)
         def _():
             greens[chunk] = driven[chunk]
@@ -139,9 +158,9 @@
             return carry
 
         lax.fori_loop(1, n_mom, send, 0)
-        columns = pl.ds(pl.multiple_of(chunk * LANES, LANES), LANES)
-        solved[0, 0, :, columns] = real.astype(jnp.bfloat16)
-        solved[1, 0, :, columns] = imag.astype(jnp.bfloat16)
+        solved[chunk, 0] = real.astype(jnp.bfloat16)
+        solved[chunk, 1] = imag.astype(jnp.bfloat16)
+        store(0, chunk).start()
 
     def form(chunk):
         settle(inbox, chunk, in_recv)
@@ -176,9 +195,9 @@
     def finish(chunk):
         settle(returned, chunk, out_recv)
         value = returned[chunk].astype(jnp.float32)
-        columns = pl.ds(pl.multiple_of(chunk * LANES, LANES), LANES)
-        sigma[0, 0, :, columns] = value[:, :share].reshape(rows, LANES)
-        sigma[1, 0, :, columns] = value[:, share:].reshape(rows, LANES)
+        sigma[chunk, 0] = value[:, :share].reshape(rows, LANES)
+        sigma[chunk, 1] = value[:, share:].reshape(rows, LANES)
+        store(1, chunk).start()
 
     def stage(step, carry):
         @pl.when(step < chunks)
@@ -204,9 +223,23 @@
 
         settle(outbox, chunk, in_send)
         settle(formed, chunk, out_send)
+        store(0, chunk).wait()
+        store(1, chunk).wait()
         return carry
 
     lax.fori_loop(0, chunks, close, 0)
+
+
+def write_out(solved, sigma, solved_out, sigma_out, sem):
+    copies = [
+        pltpu.make_async_copy(here.at[part], there.at[part], sem.at[place, part])
+        for place, (here, there) in enumerate(((sigma, sigma_out), (solved, solved_out)))
+        for part in range(2)
+    ]
+    for copy in copies:
+        copy.start()
+    for copy in copies:
+        copy.wait()
 
 
 def local(source, inverse_diag, coupling, pair_moms, pair_count, pair_weight, vertex):
@@ -214,20 +247,22 @@
     n_mom = lax.axis_size("mom")
     chunks, share = columns // LANES, rows // n_mom
     f32, bf16 = jnp.float32, jnp.bfloat16
-    smem = pl.BlockSpec(memory_space=pltpu.SMEM)
-    vmem = pl.BlockSpec(memory_space=pltpu.VMEM)
-    hbm = pl.BlockSpec(memory_space=pl.ANY)
+    hbm = pl.BlockSpec(memory_space=pltpu.HBM)
     piece = (chunks, n_mom, 2 * share, LANES)
     sems = pltpu.SemaphoreType.DMA((chunks,))
-    return pl.pallas_call(
+    results = pl.pallas_call(
         kernel,
         out_shape=(
             jax.ShapeDtypeStruct(source.shape, bf16),
             jax.ShapeDtypeStruct(source.shape, f32),
         ),
-        in_specs=[smem] * 4 + [hbm] * 3,
-        out_specs=(vmem, vmem),
+        in_specs=[hbm] * 7,
+        out_specs=(hbm, hbm),
         scratch_shapes=[
+            pltpu.SMEM(pair_moms.shape[::-1], jnp.int32),
+            pltpu.SMEM(pair_count.shape, jnp.int32),
+            pltpu.SMEM(pair_weight.shape[::-1], jnp.int32),
+            pltpu.SMEM(vertex.shape, f32),
             pltpu.VMEM((2, rows, columns), f32),
             pltpu.VMEM((2, rows, rows), f32),
             pltpu.VMEM((2, rows, rows), f32),
@@ -243,16 +278,29 @@
             pltpu.VMEM(piece[1:], f32),
             pltpu.VMEM(piece, bf16),
             pltpu.VMEM(piece, bf16),
-            pltpu.SemaphoreType.DMA((3,)),
+            pltpu.VMEM((chunks, 2, rows, LANES), bf16),
+            pltpu.VMEM((chunks, 2, rows, LANES), f32),
+            pltpu.SemaphoreType.DMA((7,)),
+            pltpu.SemaphoreType.DMA((2, chunks)),
             sems, sems, sems, sems, sems, sems,
         ],
         compiler_params=pltpu.CompilerParams(
-            collective_id=0, has_side_effects=True, vmem_limit_bytes=32 << 20
+            collective_id=0, has_side_effects=True, vmem_limit_bytes=58 << 20
         ),
     )(
         jnp.transpose(pair_moms, (2, 1, 0)), pair_count, jnp.transpose(pair_weight, (1, 0)), vertex,
         source, inverse_diag, coupling,
     )
+    return pl.pallas_call(
+        write_out,
+        out_shape=(
+            jax.ShapeDtypeStruct(source.shape, bf16),
+            jax.ShapeDtypeStruct(source.shape, f32),
+        ),
+        in_specs=[pl.BlockSpec(memory_space=pl.ANY)] * 2,
+        out_specs=(hbm, hbm),
+        scratch_shapes=[pltpu.SemaphoreType.DMA((2, 2))],
+    )(*results)
 
 
 def solution(mesh):

time: 68.6 us -> 110 us (1.60)
  the two profiles are of different devices: /device:TPU:25 before, /device:TPU:24 now
where the time goes in v2:
time: 110 us; the launch traced here: 108 us
  Pallas kernels  108 us (98%)
    pallas_call x1, Pallas kernels, local(): pl.pallas_call(kernel, out_shape=(jax.ShapeDtypeStruct(source.shape, bf16...  59.1 us
    pallas_call x1, Pallas kernels, local(): pl.pallas_call(write_out, out_shape=(jax.ShapeDtypeStruct(source.shape, b...  48.8 us

profile of v2, /device:TPU:24, one launch (start us, length us, event | category | flops | bytes accessed | tf_op | source)
XLA Modules:
  0.0 108.5 jit_solution(3020529562774099364)
XLA Ops:
  0.6 59.1 %shard_map.86 = (bf16[2,1,256,512]{3,2,1,0:T(8,128)(2,1)}, f32[2,1,256,512]{3,2,1,0:T(8,128)}) custom-call(s32[3,8,32]{2,1,0:T(8,128)} %bitcast.2, s32[32]{0:T(128)} %counts_hbm.1, s32[8,32]{1,0:T(8,128)} %bitcast.3, f32[16]{0:T(128)} %vertex_hbm.1, f32[2,1,256,512]{3,2,1,0:T(8,128)} %source_hbm.1, f32[2,1,1,256,256]{4,3,2,1,0:T(8,128)} %inverse_hbm.1, ...), custom_call_target="tpu_custom_call" | custom-call | tf_op jit(solution)/shard_map/pallas_call | solution.py:253
  59.7 48.8 %shard_map.87 = (bf16[2,1,256,512]{3,2,1,0:T(8,128)(2,1)}, f32[2,1,256,512]{3,2,1,0:T(8,128)}) custom-call(bf16[2,1,256,512]{3,2,1,0:T(8,128)(2,1)} %get-tuple-element.4.solved, f32[2,1,256,512]{3,2,1,0:T(8,128)} %get-tuple-element.5.sigma), custom_call_target="tpu_custom_call" | custom-call | tf_op jit(solution)/shard_map/pallas_call | solution.py:294

commit v3 on v2

--- a/solution.py
+++ b/solution.py
@@ -230,18 +230,6 @@
     lax.fori_loop(0, chunks, close, 0)
 
 
-def write_out(solved, sigma, solved_out, sigma_out, sem):
-    copies = [
-        pltpu.make_async_copy(here.at[part], there.at[part], sem.at[place, part])
-        for place, (here, there) in enumerate(((sigma, sigma_out), (solved, solved_out)))
-        for part in range(2)
-    ]
-    for copy in copies:
-        copy.start()
-    for copy in copies:
-        copy.wait()
-
-
 def local(source, inverse_diag, coupling, pair_moms, pair_count, pair_weight, vertex):
     rows, columns = source.shape[2], source.shape[3]
     n_mom = lax.axis_size("mom")
@@ -250,7 +238,7 @@
     hbm = pl.BlockSpec(memory_space=pltpu.HBM)
     piece = (chunks, n_mom, 2 * share, LANES)
     sems = pltpu.SemaphoreType.DMA((chunks,))
-    results = pl.pallas_call(
+    return pl.pallas_call(
         kernel,
         out_shape=(
             jax.ShapeDtypeStruct(source.shape, bf16),
@@ -291,16 +279,6 @@
         jnp.transpose(pair_moms, (2, 1, 0)), pair_count, jnp.transpose(pair_weight, (1, 0)), vertex,
         source, inverse_diag, coupling,
     )
-    return pl.pallas_call(
-        write_out,
-        out_shape=(
-            jax.ShapeDtypeStruct(source.shape, bf16),
-            jax.ShapeDtypeStruct(source.shape, f32),
-        ),
-        in_specs=[pl.BlockSpec(memory_space=pl.ANY)] * 2,
-        out_specs=(hbm, hbm),
-        scratch_shapes=[pltpu.SemaphoreType.DMA((2, 2))],
-    )(*results)
 
 
 def solution(mesh):

time: 110 us -> 64.4 us (0.59)
  the two profiles are of different devices: /device:TPU:24 before, /device:TPU:25 now
where the time goes in v3:
time: 64.4 us; the launch traced here: 64.2 us
  Pallas kernels  60.6 us (94%)
  local copies, waits for them, and re-layouts  2.93 us (5%)
  between operations  0.65 us (1%)
    pallas_call x1, Pallas kernels, local(): pl.pallas_call(kernel, out_shape=(jax.ShapeDtypeStruct(source.shape, bf16...  60.6 us
    unnamed x4, local copies, waits for them, and re-layouts  2.93 us

profile of v3, /device:TPU:25, one launch (start us, length us, event | category | flops | bytes accessed | tf_op | source)
XLA Modules:
  0.0 64.2 jit_solution(12111915738058700604)
XLA Ops:
  0.6 60.6 %shard_map.86 = (bf16[2,1,256,512]{3,2,1,0:T(8,128)(2,1)}, f32[2,1,256,512]{3,2,1,0:T(8,128)}) custom-call(s32[3,8,32]{2,1,0:T(8,128)} %bitcast.2, s32[32]{0:T(128)} %counts_hbm.1, s32[8,32]{1,0:T(8,128)} %bitcast.3, f32[16]{0:T(128)} %vertex_hbm.1, f32[2,1,256,512]{3,2,1,0:T(8,128)} %source_hbm.1, f32[2,1,1,256,256]{4,3,2,1,0:T(8,128)} %inverse_hbm.1, ...), custom_call_target="tpu_custom_call" | custom-call | tf_op jit(solution)/shard_map/pallas_call | solution.py:241
  61.3 0.0 copy-start
  61.3 2.0 %copy.11 = bf16[2,1,256,512]{3,2,1,0:T(8,128)(2,1)} copy(bf16[2,1,256,512]{3,2,1,0:T(8,128)(2,1)} %get-tuple-element.4) | data formatting | bytes 1048576
  63.3 0.0 copy-done
  63.3 1.0 %copy.12 = f32[2,1,256,512]{3,2,1,0:T(8,128)} copy(f32[2,1,256,512]{3,2,1,0:T(8,128)S(1)} %copy-done) | data formatting | bytes 2097152
Async XLA Ops:
  61.3 2.0 %copy-start = (f32[2,1,256,512]{3,2,1,0:T(8,128)S(1)}, f32[2,1,256,512]{3,2,1,0:T(8,128)}, u32[]{:S(2)}) copy-start(f32[2,1,256,512]{3,2,1,0:T(8,128)} %get-tuple-element.5) | copy-start | bytes 3145732

commit v4 on v3

--- a/solution.py
+++ b/solution.py
@@ -25,6 +25,24 @@
     real = both[:rows, :width] - both[rows:, width:]
     imag = both[:rows, width:] + both[rows:, :width]
     return real, imag
+
+
+def pack(real, imag):
+    axis = real.ndim - 1
+    lower = lax.broadcasted_iota(jnp.int32, real.shape, axis) < LANES // 2
+    return (
+        jnp.where(lower, real, pltpu.roll(imag, LANES // 2, axis)),
+        jnp.where(lower, pltpu.roll(real, LANES // 2, axis), imag),
+    )
+
+
+def packed_times(high, low, value):
+    rows = high.shape[1]
+    value_high, value_low = split(value)
+    both = dot(high, value_high) + (dot(high, value_low) + dot(low, value_high))
+    top, turned = both[:rows], pltpu.roll(both[rows:], LANES // 2, 1)
+    lower = lax.broadcasted_iota(jnp.int32, top.shape, 1) < LANES // 2
+    return top + jnp.where(lower, -turned, turned)
 
 
 def kernel(
@@ -36,7 +54,7 @@
 ):
     n_mom, n_tm = lax.axis_size("mom"), lax.axis_size("tm")
     me, turn = lax.axis_index("mom"), lax.axis_index("tm")
-    rows, chunks = driven.shape[1], driven.shape[0]
+    rows, chunks = sigma.shape[2], sigma.shape[0]
     share = rows // n_mom
     slots = moms.shape[1]
 
@@ -70,8 +88,8 @@
     def drive(chunk):
         columns = pl.ds(pl.multiple_of(chunk * LANES, LANES), LANES)
         forcing = jnp.concatenate([source[0, :, columns], source[1, :, columns]], axis=1)
-        real, imag = complex_times(left_high[...], left_low[...], forcing)
-        driven[chunk] = jnp.concatenate([real, imag], axis=1)
+        for half, value in enumerate(pack(*complex_times(left_high[...], left_low[...], forcing))):
+            driven[2 * chunk + half] = value
 
     loads[0].wait()
     for part in range(2):
@@ -126,45 +144,39 @@
         columns = pl.ds(pl.multiple_of(chunk * LANES, LANES), LANES)
         return pltpu.make_async_copy(here.at[chunk], there.at[:, 0, :, columns], store_sem.at[which, chunk])
 
-    def advance(chunk):
-        @pl.when(chunk > 0)
-        def _():
-            drive(chunk)
-
+    def advance(piece, carry):
         @pl.when(turn == 0)
         def _():
-            greens[chunk] = driven[chunk]
+            greens[piece] = driven[piece]
 
         @pl.when(turn > 0)
         def _():
-            hop(chunk).wait_recv()
-            real, imag = complex_times(step_high[...], step_low[...], entering[chunk])
-            greens[chunk] = driven[chunk] + jnp.concatenate([real, imag], axis=1)
+            hop(piece).wait_recv()
+            greens[piece] = driven[piece] + packed_times(step_high[...], step_low[...], entering[piece])
 
         @pl.when(turn < n_tm - 1)
         def _():
-            hop(chunk).start()
-
-        value = greens[chunk]
-        real, imag = value[:, :LANES], value[:, LANES:]
-        packed = jnp.concatenate(
-            [real.reshape(n_mom, share, LANES), imag.reshape(n_mom, share, LANES)], axis=1
-        )
-        outbox[chunk] = packed.astype(jnp.bfloat16)
-        inbox[chunk, me] = outbox[chunk, me]
+            hop(piece).start()
+
+        outbox[piece] = greens[piece].reshape(n_mom, share, LANES).astype(jnp.bfloat16)
+        inbox[piece, me] = outbox[piece, me]
 
         def send(step, carry):
-            scatter(chunk, lax.rem(me + step, n_mom)).start()
+            scatter(piece, lax.rem(me + step, n_mom)).start()
             return carry
 
-        lax.fori_loop(1, n_mom, send, 0)
-        solved[chunk, 0] = real.astype(jnp.bfloat16)
-        solved[chunk, 1] = imag.astype(jnp.bfloat16)
+        return lax.fori_loop(1, n_mom, send, carry)
+
+    def keep(chunk):
+        for part, value in enumerate(pack(greens[2 * chunk], greens[2 * chunk + 1])):
+            solved[chunk, part] = value
         store(0, chunk).start()
 
     def form(chunk):
-        settle(inbox, chunk, in_recv)
-        wide[...] = inbox[chunk].astype(jnp.float32)
+        for half in range(2):
+            settle(inbox, 2 * chunk + half, in_recv)
+        for part, value in enumerate(pack(*(inbox[2 * chunk + half].astype(jnp.float32) for half in range(2)))):
+            wide[:, part * share:(part + 1) * share] = value
 
         def one(step, carry):
             mom = lax.rem(me + step, n_mom)
@@ -200,9 +212,14 @@
         store(1, chunk).start()
 
     def stage(step, carry):
+        @pl.when((step > 0) & (step < chunks))
+        def _():
+            drive(step)
+
         @pl.when(step < chunks)
         def _():
-            advance(step)
+            lax.fori_loop(2 * step, 2 * step + 2, advance, 0)
+            keep(step)
 
         @pl.when((step >= 1) & (step < chunks + 1))
         def _():
@@ -216,12 +233,17 @@
 
     lax.fori_loop(0, chunks + 2, stage, 0)
 
+    def close_piece(piece, carry):
+        @pl.when(turn < n_tm - 1)
+        def _():
+            hop(piece).wait_send()
+
+        settle(outbox, piece, in_send)
+        return carry
+
+    lax.fori_loop(0, 2 * chunks, close_piece, 0)
+
     def close(chunk, carry):
-        @pl.when(turn < n_tm - 1)
-        def _():
-            hop(chunk).wait_send()
-
-        settle(outbox, chunk, in_send)
         settle(formed, chunk, out_send)
         store(0, chunk).wait()
         store(1, chunk).wait()
@@ -237,11 +259,11 @@
     f32, bf16 = jnp.float32, jnp.bfloat16
     hbm = pl.BlockSpec(memory_space=pltpu.HBM)
     piece = (chunks, n_mom, 2 * share, LANES)
-    sems = pltpu.SemaphoreType.DMA((chunks,))
-    return pl.pallas_call(
+    sems, twice = pltpu.SemaphoreType.DMA((chunks,)), pltpu.SemaphoreType.DMA((2 * chunks,))
+    greens, sigma = pl.pallas_call(
         kernel,
         out_shape=(
-            jax.ShapeDtypeStruct(source.shape, bf16),
+            jax.ShapeDtypeStruct(source.shape, f32),
             jax.ShapeDtypeStruct(source.shape, f32),
         ),
         in_specs=[hbm] * 7,
@@ -258,19 +280,19 @@
             pltpu.VMEM((2 * rows, rows), bf16),
             pltpu.VMEM((2 * rows, rows), bf16),
             pltpu.VMEM((2 * rows, rows), bf16),
-            pltpu.VMEM((chunks, rows, 2 * LANES), f32),
-            pltpu.VMEM((chunks, rows, 2 * LANES), f32),
-            pltpu.VMEM((chunks, rows, 2 * LANES), f32),
-            pltpu.VMEM(piece, bf16),
-            pltpu.VMEM(piece, bf16),
+            pltpu.VMEM((2 * chunks, rows, LANES), f32),
+            pltpu.VMEM((2 * chunks, rows, LANES), f32),
+            pltpu.VMEM((2 * chunks, rows, LANES), f32),
+            pltpu.VMEM((2 * chunks, n_mom, share, LANES), bf16),
+            pltpu.VMEM((2 * chunks, n_mom, share, LANES), bf16),
             pltpu.VMEM(piece[1:], f32),
             pltpu.VMEM(piece, bf16),
             pltpu.VMEM(piece, bf16),
-            pltpu.VMEM((chunks, 2, rows, LANES), bf16),
+            pltpu.VMEM((chunks, 2, rows, LANES), f32),
             pltpu.VMEM((chunks, 2, rows, LANES), f32),
             pltpu.SemaphoreType.DMA((7,)),
             pltpu.SemaphoreType.DMA((2, chunks)),
-            sems, sems, sems, sems, sems, sems,
+            twice, twice, twice, twice, sems, sems,
         ],
         compiler_params=pltpu.CompilerParams(
             collective_id=0, has_side_effects=True, vmem_limit_bytes=58 << 20
@@ -279,6 +301,7 @@
         jnp.transpose(pair_moms, (2, 1, 0)), pair_count, jnp.transpose(pair_weight, (1, 0)), vertex,
         source, inverse_diag, coupling,
     )
+    return greens.astype(bf16), sigma
 
 
 def solution(mesh):

time: 64.4 us -> 62.2 us (0.966)
  the two profiles are of different devices: /device:TPU:25 before, /device:TPU:24 now
where the time goes in v4:
time: 62.2 us; the launch traced here: 61.8 us
  Pallas kernels  58 us (93%)
  other arithmetic  2.17 us (3%)
  local copies, waits for them, and re-layouts  0.97 us (2%)
  between operations  0.65 us (1%)
    pallas_call x1, Pallas kernels, local(): pl.pallas_call(kernel, out_shape=(jax.ShapeDtypeStruct(source.shape, f32)...  58 us
    convert_element_type x1, other arithmetic, local(): return (greens.astype(bf16), sigma)  2.17 us

profile of v4, /device:TPU:24, one launch (start us, length us, event | category | flops | bytes accessed | tf_op | source)
XLA Modules:
  0.0 61.8 jit_solution(5019127356355523846)
XLA Ops:
  0.6 58.0 %shard_map.86 = (f32[2,1,256,512]{3,2,1,0:T(8,128)}, f32[2,1,256,512]{3,2,1,0:T(8,128)}) custom-call(s32[3,8,32]{2,1,0:T(8,128)} %bitcast.2, s32[32]{0:T(128)} %counts_hbm.1, s32[8,32]{1,0:T(8,128)} %bitcast.3, f32[16]{0:T(128)} %vertex_hbm.1, f32[2,1,256,512]{3,2,1,0:T(8,128)} %source_hbm.1, f32[2,1,1,256,256]{4,3,2,1,0:T(8,128)} %inverse_hbm.1, ...), custom_call_target="tpu_custom_call" | custom-call | tf_op jit(solution)/shard_map/pallas_call | solution.py:263
  58.6 0.0 copy-start
  58.6 2.2 %convert_element_type.3 = bf16[2,1,256,512]{3,2,1,0:T(8,128)(2,1)} convert(f32[2,1,256,512]{3,2,1,0:T(8,128)} %get-tuple-element.4) | non-fusion elementwise | flops 262144 | bytes 1572864 | tf_op jit(solution)/shard_map/convert_element_type | solution.py:304
  60.8 0.0 copy-done
  60.8 1.0 %copy.10 = f32[2,1,256,512]{3,2,1,0:T(8,128)} copy(f32[2,1,256,512]{3,2,1,0:T(8,128)S(1)} %copy-done) | data formatting | bytes 2097152
Async XLA Ops:
  58.6 2.2 %copy-start = (f32[2,1,256,512]{3,2,1,0:T(8,128)S(1)}, f32[2,1,256,512]{3,2,1,0:T(8,128)}, u32[]{:S(2)}) copy-start(f32[2,1,256,512]{3,2,1,0:T(8,128)} %get-tuple-element.9) | copy-start | bytes 3145732

commit v5 on v4

--- a/solution.py
+++ b/solution.py
@@ -18,13 +18,19 @@
     return jnp.dot(left, right, preferred_element_type=jnp.float32)
 
 
-def complex_times(high, low, value):
-    rows, width = high.shape[1], value.shape[1] // 2
-    value_high, value_low = split(value)
-    both = dot(high, value_high) + (dot(high, value_low) + dot(low, value_high))
+def product(high, low, value_high, value_low):
+    return dot(high, value_high) + (dot(high, value_low) + dot(low, value_high))
+
+
+def join(both):
+    rows, width = both.shape[0] // 2, both.shape[1] // 2
     real = both[:rows, :width] - both[rows:, width:]
     imag = both[:rows, width:] + both[rows:, :width]
     return real, imag
+
+
+def complex_times(high, low, value):
+    return join(product(high, low, *split(value)))
 
 
 def pack(real, imag):
@@ -38,25 +44,30 @@
 
 def packed_times(high, low, value):
     rows = high.shape[1]
-    value_high, value_low = split(value)
-    both = dot(high, value_high) + (dot(high, value_low) + dot(low, value_high))
-    top, turned = both[:rows], pltpu.roll(both[rows:], LANES // 2, 1)
-    lower = lax.broadcasted_iota(jnp.int32, top.shape, 1) < LANES // 2
-    return top + jnp.where(lower, -turned, turned)
+    both = product(high, low, *split(value))
+    lower = lax.broadcasted_iota(jnp.int32, (rows, LANES), 1) < LANES // 2
+    blocks = []
+    for at in range(0, value.shape[1], LANES):
+        turned = pltpu.roll(both[rows:, at:at + LANES], LANES // 2, 1)
+        blocks.append(both[:rows, at:at + LANES] + jnp.where(lower, -turned, turned))
+    return blocks
 
 
 def kernel(
     moms_hbm, counts_hbm, weights_hbm, vertex_hbm, source_hbm, inverse_hbm, coupling_hbm,
     solved_hbm, sigma_hbm,
-    moms, counts, weights, vertex, source, inverse, coupling, left_high, left_low, step_high, step_low, driven, entering, greens,
+    moms, counts, weights, vertex, source, inverse, coupling, left_high, left_low, own_high, own_low, pair_high, pair_low, step_high, step_low,
+    driven, lent, entering, greens,
     outbox, inbox, wide, formed, returned, solved, sigma,
-    load_sem, store_sem, hop_send, hop_recv, in_send, in_recv, out_send, out_recv,
+    load_sem, store_sem, pair_send, pair_recv, lend_send, lend_recv, pass_send, hop_send, hop_recv, in_send, in_recv, out_send, out_recv,
 ):
     n_mom, n_tm = lax.axis_size("mom"), lax.axis_size("tm")
     me, turn = lax.axis_index("mom"), lax.axis_index("tm")
     rows, chunks = sigma.shape[2], sigma.shape[0]
     share = rows // n_mom
     slots = moms.shape[1]
+    core, plane, planes = lax.rem(turn, 2), turn // 2, n_tm // 2
+    partner = turn + 1 - 2 * core
 
     loads = [
         pltpu.make_async_copy(here, there, load_sem.at[place])
@@ -82,7 +93,7 @@
 
     lax.fori_loop(1, n_mom, greet, 0)
 
-    for other in (lax.rem(turn + 1, n_tm), lax.rem(turn + n_tm - 1, n_tm)):
+    for other in (partner, lax.rem(turn + 2, n_tm), lax.rem(turn + n_tm - 2, n_tm)):
         pl.semaphore_signal(barrier, inc=1, device_id={"mom": me, "tm": other}, device_id_type=MESH)
 
     def drive(chunk):
@@ -100,26 +111,85 @@
     drive(0)
     loads[2].wait()
 
-    @pl.when(turn > 0)
+    def keep_matrix(high_ref, low_ref, matrix):
+        for part in range(2):
+            high, low = split(matrix[part])
+            high_ref[part * rows:(part + 1) * rows, :] = high
+            low_ref[part * rows:(part + 1) * rows, :] = low
+
+    @pl.when((plane > 0) | (core == 1))
     def _():
-        step = complex_times(
+        keep_matrix(own_high, own_low, complex_times(
             left_high[...], left_low[...], jnp.concatenate([coupling[0], coupling[1]], axis=1)
-        )
-        for part in range(2):
-            high, low = split(step[part])
-            step_high[part * rows:(part + 1) * rows, :] = high
-            step_low[part * rows:(part + 1) * rows, :] = low
+        ))
 
     for load in loads[3:]:
         load.wait()
-    pl.semaphore_wait(barrier, n_mom + 1)
-
-    def hop(chunk):
+    pl.semaphore_wait(barrier, n_mom + 2)
+
+    def to(other, src, dst, send_sem, recv_sem):
         return pltpu.make_async_remote_copy(
-            src_ref=greens.at[chunk], dst_ref=entering.at[chunk],
-            send_sem=hop_send.at[chunk], recv_sem=hop_recv.at[chunk],
-            device_id={"mom": me, "tm": lax.rem(turn + 1, n_tm)}, device_id_type=MESH,
+            src_ref=src, dst_ref=dst, send_sem=send_sem, recv_sem=recv_sem,
+            device_id={"mom": me, "tm": other}, device_id_type=MESH,
         )
+
+    def lend(piece):
+        return to(partner, driven.at[piece], lent.at[piece], lend_send.at[piece], lend_recv.at[piece])
+
+    def hop(piece):
+        return to(
+            lax.rem(turn + 2, n_tm), greens.at[piece], entering.at[piece], hop_send.at[piece], hop_recv.at[piece]
+        )
+
+    def forward(piece):
+        return to(partner, entering.at[piece], entering.at[piece], pass_send.at[piece], hop_recv.at[piece])
+
+    pairs = (
+        to(partner, own_high, pair_high, pair_send.at[0], pair_recv.at[0]),
+        to(partner, own_low, pair_low, pair_send.at[1], pair_recv.at[1]),
+    )
+
+    @pl.when(core == 0)
+    def _():
+        for half in range(2):
+            lend(half).start()
+
+        @pl.when(plane > 0)
+        def _():
+            for pair in pairs:
+                pair.start()
+            step_high[...] = own_high[...]
+            step_low[...] = own_low[...]
+
+        def drive_and_lend(chunk, carry):
+            drive(chunk)
+            for half in range(2):
+                lend(2 * chunk + half).start()
+            return carry
+
+        lax.fori_loop(1, chunks, drive_and_lend, 0)
+
+    @pl.when((core == 1) & (plane > 0))
+    def _():
+        for pair in pairs:
+            pair.wait_recv()
+        both = product(
+            own_high[...], own_low[...],
+            jnp.concatenate([pair_high[:rows, :], pair_high[rows:, :]], axis=1),
+            jnp.concatenate([pair_low[:rows, :], pair_low[rows:, :]], axis=1),
+        )
+        keep_matrix(step_high, step_low, join(both))
+
+    def compose(chunk):
+        @pl.when(chunk > 0)
+        def _():
+            drive(chunk)
+
+        for half in range(2):
+            lend(2 * chunk + half).wait_recv()
+        value = jnp.concatenate([lent[2 * chunk], lent[2 * chunk + 1]], axis=1)
+        for half, block in enumerate(packed_times(own_high[...], own_low[...], value)):
+            driven[2 * chunk + half] = driven[2 * chunk + half] + block
 
     def scatter(chunk, other):
         return pltpu.make_async_remote_copy(
@@ -145,16 +215,22 @@
         return pltpu.make_async_copy(here.at[chunk], there.at[:, 0, :, columns], store_sem.at[which, chunk])
 
     def advance(piece, carry):
-        @pl.when(turn == 0)
+        @pl.when(plane == 0)
         def _():
             greens[piece] = driven[piece]
 
-        @pl.when(turn > 0)
+        @pl.when(plane > 0)
         def _():
             hop(piece).wait_recv()
-            greens[piece] = driven[piece] + packed_times(step_high[...], step_low[...], entering[piece])
-
-        @pl.when(turn < n_tm - 1)
+
+            @pl.when(core == 1)
+            def _():
+                forward(piece).start()
+
+            [block] = packed_times(step_high[...], step_low[...], entering[piece])
+            greens[piece] = driven[piece] + block
+
+        @pl.when((core == 1) & (plane < planes - 1))
         def _():
             hop(piece).start()
 
@@ -212,9 +288,9 @@
         store(1, chunk).start()
 
     def stage(step, carry):
-        @pl.when((step > 0) & (step < chunks))
-        def _():
-            drive(step)
+        @pl.when((core == 1) & (step < chunks))
+        def _():
+            compose(step)
 
         @pl.when(step < chunks)
         def _():
@@ -234,7 +310,15 @@
     lax.fori_loop(0, chunks + 2, stage, 0)
 
     def close_piece(piece, carry):
-        @pl.when(turn < n_tm - 1)
+        @pl.when(core == 0)
+        def _():
+            lend(piece).wait_send()
+
+        @pl.when((core == 1) & (plane > 0))
+        def _():
+            forward(piece).wait_send()
+
+        @pl.when((core == 1) & (plane < planes - 1))
         def _():
             hop(piece).wait_send()
 
@@ -242,6 +326,11 @@
         return carry
 
     lax.fori_loop(0, 2 * chunks, close_piece, 0)
+
+    @pl.when((core == 0) & (plane > 0))
+    def _():
+        for pair in pairs:
+            pair.wait_send()
 
     def close(chunk, carry):
         settle(formed, chunk, out_send)
@@ -276,10 +365,8 @@
             pltpu.VMEM((2, rows, columns), f32),
             pltpu.VMEM((2, rows, rows), f32),
             pltpu.VMEM((2, rows, rows), f32),
-            pltpu.VMEM((2 * rows, rows), bf16),
-            pltpu.VMEM((2 * rows, rows), bf16),
-            pltpu.VMEM((2 * rows, rows), bf16),
-            pltpu.VMEM((2 * rows, rows), bf16),
+            *[pltpu.VMEM((2 * rows, rows), bf16) for _ in range(8)],
+            pltpu.VMEM((2 * chunks, rows, LANES), f32),
             pltpu.VMEM((2 * chunks, rows, LANES), f32),
             pltpu.VMEM((2 * chunks, rows, LANES), f32),
             pltpu.VMEM((2 * chunks, rows, LANES), f32),
@@ -292,7 +379,9 @@
             pltpu.VMEM((chunks, 2, rows, LANES), f32),
             pltpu.SemaphoreType.DMA((7,)),
             pltpu.SemaphoreType.DMA((2, chunks)),
-            twice, twice, twice, twice, sems, sems,
+            pltpu.SemaphoreType.DMA((2,)),
+            pltpu.SemaphoreType.DMA((2,)),
+            twice, twice, twice, twice, twice, twice, twice, sems, sems,
         ],
         compiler_params=pltpu.CompilerParams(
             collective_id=0, has_side_effects=True, vmem_limit_bytes=58 << 20

time: 62.2 us -> 57.9 us (0.931)
  Pallas kernels: 58 us -> 54 us
    pallas_call x1, Pallas kernels: 58 us -> 54 us  [local(): pl.pallas_call(kernel, out_shape=(jax.ShapeDtypeStruct(source.shape, f32)...]
where the time goes in v5:
time: 57.9 us; the launch traced here: 57.8 us
  Pallas kernels  54 us (93%)
  other arithmetic  2.17 us (4%)
  local copies, waits for them, and re-layouts  0.97 us (2%)
  between operations  0.65 us (1%)
    pallas_call x1, Pallas kernels, local(): pl.pallas_call(kernel, out_shape=(jax.ShapeDtypeStruct(source.shape, f32)...  54 us
    convert_element_type x1, other arithmetic, local(): return (greens.astype(bf16), sigma)  2.17 us

profile of v5, /device:TPU:24, one launch (start us, length us, event | category | flops | bytes accessed | tf_op | source)
XLA Modules:
  0.0 57.8 jit_solution(5937732398637330365)
XLA Ops:
  0.6 54.0 %shard_map.86 = (f32[2,1,256,512]{3,2,1,0:T(8,128)}, f32[2,1,256,512]{3,2,1,0:T(8,128)}) custom-call(s32[3,8,32]{2,1,0:T(8,128)} %bitcast.2, s32[32]{0:T(128)} %counts_hbm.1, s32[8,32]{1,0:T(8,128)} %bitcast.3, f32[16]{0:T(128)} %vertex_hbm.1, f32[2,1,256,512]{3,2,1,0:T(8,128)} %source_hbm.1, f32[2,1,1,256,256]{4,3,2,1,0:T(8,128)} %inverse_hbm.1, ...), custom_call_target="tpu_custom_call" | custom-call | tf_op jit(solution)/shard_map/pallas_call | solution.py:352
  54.6 0.0 copy-start
  54.6 2.2 %convert_element_type.3 = bf16[2,1,256,512]{3,2,1,0:T(8,128)(2,1)} convert(f32[2,1,256,512]{3,2,1,0:T(8,128)} %get-tuple-element.4) | non-fusion elementwise | flops 262144 | bytes 1572864 | tf_op jit(solution)/shard_map/convert_element_type | solution.py:393
  56.8 0.0 copy-done
  56.8 1.0 %copy.10 = f32[2,1,256,512]{3,2,1,0:T(8,128)} copy(f32[2,1,256,512]{3,2,1,0:T(8,128)S(1)} %copy-done) | data formatting | bytes 2097152
Async XLA Ops:
  54.6 2.2 %copy-start = (f32[2,1,256,512]{3,2,1,0:T(8,128)S(1)}, f32[2,1,256,512]{3,2,1,0:T(8,128)}, u32[]{:S(2)}) copy-start(f32[2,1,256,512]{3,2,1,0:T(8,128)} %get-tuple-element.9) | copy-start | bytes 3145732

commit v6 on v5

--- a/solution.py
+++ b/solution.py
@@ -68,6 +68,8 @@
     slots = moms.shape[1]
     core, plane, planes = lax.rem(turn, 2), turn // 2, n_tm // 2
     partner = turn + 1 - 2 * core
+    first, last = plane == 0, plane == planes - 1
+    ahead = 2 * (planes - 1)
 
     loads = [
         pltpu.make_async_copy(here, there, load_sem.at[place])
@@ -96,6 +98,23 @@
     for other in (partner, lax.rem(turn + 2, n_tm), lax.rem(turn + n_tm - 2, n_tm)):
         pl.semaphore_signal(barrier, inc=1, device_id={"mom": me, "tm": other}, device_id_type=MESH)
 
+    def greet_helper(shift):
+        def greet_one(other, carry):
+            pl.semaphore_signal(
+                barrier, inc=1, device_id={"mom": other, "tm": turn + shift}, device_id_type=MESH
+            )
+            return carry
+
+        lax.fori_loop(0, n_mom, greet_one, 0)
+
+    @pl.when(first)
+    def _():
+        greet_helper(ahead)
+
+    @pl.when(last)
+    def _():
+        greet_helper(-ahead)
+
     def drive(chunk):
         columns = pl.ds(pl.multiple_of(chunk * LANES, LANES), LANES)
         forcing = jnp.concatenate([source[0, :, columns], source[1, :, columns]], axis=1)
@@ -125,7 +144,14 @@
 
     for load in loads[3:]:
         load.wait()
-    pl.semaphore_wait(barrier, n_mom + 2)
+
+    @pl.when(first | last)
+    def _():
+        pl.semaphore_wait(barrier, 2 * n_mom + 2)
+
+    @pl.when(jnp.logical_not(first | last))
+    def _():
+        pl.semaphore_wait(barrier, n_mom + 2)
 
     def to(other, src, dst, send_sem, recv_sem):
         return pltpu.make_async_remote_copy(
@@ -191,23 +217,21 @@
         for half, block in enumerate(packed_times(own_high[...], own_low[...], value)):
             driven[2 * chunk + half] = driven[2 * chunk + half] + block
 
-    def scatter(chunk, other):
-        return pltpu.make_async_remote_copy(
-            src_ref=outbox.at[chunk, other], dst_ref=inbox.at[chunk, me],
-            send_sem=in_send.at[chunk], recv_sem=in_recv.at[chunk],
-            device_id={"mom": other, "tm": turn}, device_id_type=MESH,
-        )
-
-    def collect(chunk, other):
-        return pltpu.make_async_remote_copy(
-            src_ref=formed.at[chunk, other], dst_ref=returned.at[chunk, me],
-            send_sem=out_send.at[chunk], recv_sem=out_recv.at[chunk],
-            device_id={"mom": other, "tm": turn}, device_id_type=MESH,
-        )
-
-    def settle(buffer, chunk, sem):
-        block = buffer.at[chunk, pl.ds(0, n_mom - 1)]
-        pltpu.make_async_copy(block, block, sem.at[chunk]).wait()
+    def send(src, dst, send_sem, recv_sem, other, there):
+        pltpu.make_async_remote_copy(
+            src_ref=src, dst_ref=dst, send_sem=send_sem, recv_sem=recv_sem,
+            device_id={"mom": other, "tm": there}, device_id_type=MESH,
+        ).start()
+
+    def settle(block, sem):
+        pltpu.make_async_copy(block, block, sem).wait()
+
+    def others(body):
+        def one(step, carry):
+            body(lax.rem(me + step, n_mom))
+            return carry
+
+        return one
 
     def store(which, chunk):
         here, there = ((solved, solved_hbm), (sigma, sigma_hbm))[which]
@@ -234,24 +258,54 @@
         def _():
             hop(piece).start()
 
-        outbox[piece] = greens[piece].reshape(n_mom, share, LANES).astype(jnp.bfloat16)
-        inbox[piece, me] = outbox[piece, me]
-
-        def send(step, carry):
-            scatter(piece, lax.rem(me + step, n_mom)).start()
-            return carry
-
-        return lax.fori_loop(1, n_mom, send, carry)
+        chunk, half = piece // 2, lax.rem(piece, 2)
+        outbox[chunk, :, half] = greens[piece].reshape(n_mom, share, LANES).astype(jnp.bfloat16)
+        given = last & (chunk == chunks - 1)
+
+        @pl.when(jnp.logical_not(given))
+        def _():
+            inbox[chunk, me, half] = outbox[chunk, me, half]
+
+        @pl.when(chunk == 0)
+        def _():
+            lax.fori_loop(1, n_mom, others(lambda other: send(
+                outbox.at[0, other, half], inbox.at[0, me, half], in_send.at[half], in_recv.at[half], other, turn
+            )), 0)
+
+        @pl.when((chunk > 0) & (half == 1) & jnp.logical_not(given))
+        def _():
+            lax.fori_loop(1, n_mom, others(lambda other: send(
+                outbox.at[chunk, other], inbox.at[chunk, me], in_send.at[chunk + 1], in_recv.at[chunk + 1], other, turn
+            )), 0)
+
+        @pl.when((half == 1) & given)
+        def _():
+            lax.fori_loop(0, n_mom, others(lambda other: send(
+                outbox.at[chunk, other], inbox.at[chunks, me], in_send.at[chunk + 1], in_recv.at[chunks + 1],
+                other, lax.rem(turn + 2, n_tm),
+            )), 0)
+
+        return carry
 
     def keep(chunk):
         for part, value in enumerate(pack(greens[2 * chunk], greens[2 * chunk + 1])):
-            solved[chunk, part] = value
+            solved[chunk, part] = value.astype(jnp.bfloat16)
         store(0, chunk).start()
 
-    def form(chunk):
-        for half in range(2):
-            settle(inbox, 2 * chunk + half, in_recv)
-        for part, value in enumerate(pack(*(inbox[2 * chunk + half].astype(jnp.float32) for half in range(2)))):
+    def form(chunk, handed):
+        if handed:
+            settle(inbox.at[chunk], in_recv.at[chunk + 1])
+        else:
+            @pl.when(chunk == 0)
+            def _():
+                for half in range(2):
+                    settle(inbox.at[0, pl.ds(0, n_mom - 1), half], in_recv.at[half])
+
+            @pl.when(chunk > 0)
+            def _():
+                settle(inbox.at[chunk, pl.ds(0, n_mom - 1)], in_recv.at[chunk + 1])
+
+        for part, value in enumerate(pack(*(inbox[chunk, :, half].astype(jnp.float32) for half in range(2)))):
             wide[:, part * share:(part + 1) * share] = value
 
         def one(step, carry):
@@ -271,17 +325,35 @@
                 total_imag = total_imag + factor * (prod_imag * cr - prod_real * ci)
             formed[chunk, mom] = jnp.concatenate([total_real, total_imag], axis=0).astype(jnp.bfloat16)
 
-            @pl.when(step < n_mom)
-            def _():
-                collect(chunk, mom).start()
+            if handed:
+                send(
+                    formed.at[chunk, mom], returned.at[chunks - 1, me], out_send.at[chunk], out_recv.at[chunks - 1],
+                    mom, turn + ahead,
+                )
+            else:
+                @pl.when(step < n_mom)
+                def _():
+                    send(
+                        formed.at[chunk, mom], returned.at[chunk, me], out_send.at[chunk], out_recv.at[chunk], mom, turn
+                    )
 
             return carry
 
         lax.fori_loop(1, n_mom + 1, one, 0)
-        returned[chunk, me] = formed[chunk, me]
+        if not handed:
+            returned[chunk, me] = formed[chunk, me]
 
     def finish(chunk):
-        settle(returned, chunk, out_recv)
+        given = last & (chunk == chunks - 1)
+
+        @pl.when(given)
+        def _():
+            settle(returned.at[chunk], out_recv.at[chunk])
+
+        @pl.when(jnp.logical_not(given))
+        def _():
+            settle(returned.at[chunk, pl.ds(0, n_mom - 1)], out_recv.at[chunk])
+
         value = returned[chunk].astype(jnp.float32)
         sigma[chunk, 0] = value[:, :share].reshape(rows, LANES)
         sigma[chunk, 1] = value[:, share:].reshape(rows, LANES)
@@ -297,9 +369,9 @@
             lax.fori_loop(2 * step, 2 * step + 2, advance, 0)
             keep(step)
 
-        @pl.when((step >= 1) & (step < chunks + 1))
-        def _():
-            form(step - 1)
+        @pl.when((step >= 1) & ((step < chunks) | ((step == chunks) & jnp.logical_not(last))))
+        def _():
+            form(step - 1, False)
 
         @pl.when(step >= 2)
         def _():
@@ -308,6 +380,10 @@
         return carry
 
     lax.fori_loop(0, chunks + 2, stage, 0)
+
+    @pl.when(first)
+    def _():
+        form(chunks, True)
 
     def close_piece(piece, carry):
         @pl.when(core == 0)
@@ -322,7 +398,6 @@
         def _():
             hop(piece).wait_send()
 
-        settle(outbox, piece, in_send)
         return carry
 
     lax.fori_loop(0, 2 * chunks, close_piece, 0)
@@ -333,12 +408,55 @@
             pair.wait_send()
 
     def close(chunk, carry):
-        settle(formed, chunk, out_send)
+        given = last & (chunk == chunks - 1)
+
+        @pl.when(chunk == 0)
+        def _():
+            for half in range(2):
+                settle(outbox.at[0, pl.ds(0, n_mom - 1), half], in_send.at[half])
+
+        @pl.when((chunk > 0) & jnp.logical_not(given))
+        def _():
+            settle(outbox.at[chunk, pl.ds(0, n_mom - 1)], in_send.at[chunk + 1])
+
+        @pl.when(given)
+        def _():
+            settle(outbox.at[chunk], in_send.at[chunk + 1])
+
+        @pl.when(jnp.logical_not(given))
+        def _():
+            settle(formed.at[chunk, pl.ds(0, n_mom - 1)], out_send.at[chunk])
+
         store(0, chunk).wait()
         store(1, chunk).wait()
         return carry
 
     lax.fori_loop(0, chunks, close, 0)
+
+    @pl.when(first)
+    def _():
+        settle(formed.at[chunks], out_send.at[chunks])
+
+
+def write_out(solved, sigma, solved_out, sigma_out, solved_held, sigma_held, in_sem, out_sem):
+    blocks = in_sem.shape[2]
+    height = solved_held.shape[1] // blocks
+    moves = []
+    for place, (src, held, dst) in enumerate(((sigma, sigma_held, sigma_out), (solved, solved_held, solved_out))):
+        for part in range(2):
+            for block in range(blocks):
+                span = pl.ds(block * height, height)
+                moves.append((
+                    pltpu.make_async_copy(src.at[part, 0, span], held.at[part, span], in_sem.at[place, part, block]),
+                    pltpu.make_async_copy(held.at[part, span], dst.at[part, 0, span], out_sem.at[place, part, block]),
+                ))
+    for arrive, _ in moves:
+        arrive.start()
+    for arrive, leave in moves:
+        arrive.wait()
+        leave.start()
+    for _, leave in moves:
+        leave.wait()
 
 
 def local(source, inverse_diag, coupling, pair_moms, pair_count, pair_weight, vertex):
@@ -348,11 +466,11 @@
     f32, bf16 = jnp.float32, jnp.bfloat16
     hbm = pl.BlockSpec(memory_space=pltpu.HBM)
     piece = (chunks, n_mom, 2 * share, LANES)
-    sems, twice = pltpu.SemaphoreType.DMA((chunks,)), pltpu.SemaphoreType.DMA((2 * chunks,))
-    greens, sigma = pl.pallas_call(
+    twice = pltpu.SemaphoreType.DMA((2 * chunks,))
+    results = pl.pallas_call(
         kernel,
         out_shape=(
-            jax.ShapeDtypeStruct(source.shape, f32),
+            jax.ShapeDtypeStruct(source.shape, bf16),
             jax.ShapeDtypeStruct(source.shape, f32),
         ),
         in_specs=[hbm] * 7,
@@ -370,18 +488,19 @@
             pltpu.VMEM((2 * chunks, rows, LANES), f32),
             pltpu.VMEM((2 * chunks, rows, LANES), f32),
             pltpu.VMEM((2 * chunks, rows, LANES), f32),
-            pltpu.VMEM((2 * chunks, n_mom, share, LANES), bf16),
-            pltpu.VMEM((2 * chunks, n_mom, share, LANES), bf16),
+            pltpu.VMEM((chunks, n_mom, 2, share, LANES), bf16),
+            pltpu.VMEM((chunks + 1, n_mom, 2, share, LANES), bf16),
             pltpu.VMEM(piece[1:], f32),
+            pltpu.VMEM((chunks + 1, *piece[1:]), bf16),
             pltpu.VMEM(piece, bf16),
-            pltpu.VMEM(piece, bf16),
-            pltpu.VMEM((chunks, 2, rows, LANES), f32),
+            pltpu.VMEM((chunks, 2, rows, LANES), bf16),
             pltpu.VMEM((chunks, 2, rows, LANES), f32),
             pltpu.SemaphoreType.DMA((7,)),
             pltpu.SemaphoreType.DMA((2, chunks)),
             pltpu.SemaphoreType.DMA((2,)),
             pltpu.SemaphoreType.DMA((2,)),
-            twice, twice, twice, twice, twice, twice, twice, sems, sems,
+            twice, twice, twice, twice, twice,
+            *[pltpu.SemaphoreType.DMA((chunks + extra,)) for extra in (1, 2, 1, 0)],
         ],
         compiler_params=pltpu.CompilerParams(
             collective_id=0, has_side_effects=True, vmem_limit_bytes=58 << 20
@@ -390,7 +509,19 @@
         jnp.transpose(pair_moms, (2, 1, 0)), pair_count, jnp.transpose(pair_weight, (1, 0)), vertex,
         source, inverse_diag, coupling,
     )
-    return greens.astype(bf16), sigma
+    blocks = 4
+    return pl.pallas_call(
+        write_out,
+        out_shape=[jax.ShapeDtypeStruct(result.shape, result.dtype) for result in results],
+        in_specs=[hbm] * 2,
+        out_specs=(hbm, hbm),
+        scratch_shapes=[
+            pltpu.VMEM((2, rows, columns), bf16),
+            pltpu.VMEM((2, rows, columns), f32),
+            pltpu.SemaphoreType.DMA((2, 2, blocks)),
+            pltpu.SemaphoreType.DMA((2, 2, blocks)),
+        ],
+    )(*results)
 
 
 def solution(mesh):

time: 57.9 us -> 63.3 us (1.093)
  Pallas kernels: 54 us -> 62.5 us
  other arithmetic: 2.17 us -> 0 us
  local copies, waits for them, and re-layouts: 0.97 us -> 0 us
    pallas_call x1 -> x2, Pallas kernels: 54 us -> 62.5 us  [the longest x1 60.1 us: local(): pl.pallas_call(kernel, out_shape=(jax.ShapeDtypeStruct(source.shape, bf16...]
    convert_element_type x1 -> x0, other arithmetic: 2.17 us -> none  [local(): return (greens.astype(bf16), sigma)]
    unnamed x3 -> x0, local copies, waits for them, and re-layouts: 0.97 us -> none
where the time goes in v6:
time: 63.3 us; the launch traced here: 63.1 us
  Pallas kernels  62.5 us (99%)
  between operations  0.64 us (1%)
    pallas_call x1, Pallas kernels, local(): pl.pallas_call(kernel, out_shape=(jax.ShapeDtypeStruct(source.shape, bf16...  60.1 us
    pallas_call x1, Pallas kernels, local(): pl.pallas_call(write_out, out_shape=[jax.ShapeDtypeStruct(result.shape, r...  2.39 us

profile of v6, /device:TPU:24, one launch (start us, length us, event | category | flops | bytes accessed | tf_op | source)
XLA Modules:
  0.0 63.1 jit_solution(5221451354574114519)
XLA Ops:
  0.6 60.1 %shard_map.86 = (bf16[2,1,256,512]{3,2,1,0:T(8,128)(2,1)}, f32[2,1,256,512]{3,2,1,0:T(8,128)}) custom-call(s32[3,8,32]{2,1,0:T(8,128)} %bitcast.2, s32[32]{0:T(128)} %counts_hbm.1, s32[8,32]{1,0:T(8,128)} %bitcast.3, f32[16]{0:T(128)} %vertex_hbm.1, f32[2,1,256,512]{3,2,1,0:T(8,128)} %source_hbm.1, f32[2,1,1,256,256]{4,3,2,1,0:T(8,128)} %inverse_hbm.1, ...), custom_call_target="tpu_custom_call" | custom-call | tf_op jit(solution)/shard_map/pallas_call | solution.py:470
  60.7 2.4 %shard_map.87 = (bf16[2,1,256,512]{3,2,1,0:T(8,128)(2,1)}, f32[2,1,256,512]{3,2,1,0:T(8,128)}) custom-call(bf16[2,1,256,512]{3,2,1,0:T(8,128)(2,1)} %get-tuple-element.4.solved, f32[2,1,256,512]{3,2,1,0:T(8,128)} %get-tuple-element.5.sigma), custom_call_target="tpu_custom_call" | custom-call | tf_op jit(solution)/shard_map/pallas_call | solution.py:513

commit v7 on v6

--- a/solution.py
+++ b/solution.py
@@ -7,6 +7,7 @@
 
 MESH = pl.DeviceIdType.MESH
 LANES = 128
+HANDED = 0
 
 
 def split(value):
@@ -98,23 +99,6 @@
     for other in (partner, lax.rem(turn + 2, n_tm), lax.rem(turn + n_tm - 2, n_tm)):
         pl.semaphore_signal(barrier, inc=1, device_id={"mom": me, "tm": other}, device_id_type=MESH)
 
-    def greet_helper(shift):
-        def greet_one(other, carry):
-            pl.semaphore_signal(
-                barrier, inc=1, device_id={"mom": other, "tm": turn + shift}, device_id_type=MESH
-            )
-            return carry
-
-        lax.fori_loop(0, n_mom, greet_one, 0)
-
-    @pl.when(first)
-    def _():
-        greet_helper(ahead)
-
-    @pl.when(last)
-    def _():
-        greet_helper(-ahead)
-
     def drive(chunk):
         columns = pl.ds(pl.multiple_of(chunk * LANES, LANES), LANES)
         forcing = jnp.concatenate([source[0, :, columns], source[1, :, columns]], axis=1)
@@ -145,13 +129,7 @@
     for load in loads[3:]:
         load.wait()
 
-    @pl.when(first | last)
-    def _():
-        pl.semaphore_wait(barrier, 2 * n_mom + 2)
-
-    @pl.when(jnp.logical_not(first | last))
-    def _():
-        pl.semaphore_wait(barrier, n_mom + 2)
+    pl.semaphore_wait(barrier, n_mom + 2)
 
     def to(other, src, dst, send_sem, recv_sem):
         return pltpu.make_async_remote_copy(
@@ -260,28 +238,23 @@
 
         chunk, half = piece // 2, lax.rem(piece, 2)
         outbox[chunk, :, half] = greens[piece].reshape(n_mom, share, LANES).astype(jnp.bfloat16)
-        given = last & (chunk == chunks - 1)
+        given = last & (chunk == HANDED)
 
         @pl.when(jnp.logical_not(given))
         def _():
             inbox[chunk, me, half] = outbox[chunk, me, half]
 
-        @pl.when(chunk == 0)
+        @pl.when(jnp.logical_not(given))
         def _():
             lax.fori_loop(1, n_mom, others(lambda other: send(
-                outbox.at[0, other, half], inbox.at[0, me, half], in_send.at[half], in_recv.at[half], other, turn
+                outbox.at[chunk, other, half], inbox.at[chunk, me, half], in_send.at[chunk], in_recv.at[chunk],
+                other, turn,
             )), 0)
 
-        @pl.when((chunk > 0) & (half == 1) & jnp.logical_not(given))
-        def _():
-            lax.fori_loop(1, n_mom, others(lambda other: send(
-                outbox.at[chunk, other], inbox.at[chunk, me], in_send.at[chunk + 1], in_recv.at[chunk + 1], other, turn
-            )), 0)
-
-        @pl.when((half == 1) & given)
+        @pl.when(given)
         def _():
             lax.fori_loop(0, n_mom, others(lambda other: send(
-                outbox.at[chunk, other], inbox.at[chunks, me], in_send.at[chunk + 1], in_recv.at[chunks + 1],
+                outbox.at[chunk, other, half], inbox.at[chunks, me, half], in_send.at[chunk], in_recv.at[chunks],
                 other, lax.rem(turn + 2, n_tm),
             )), 0)
 
@@ -294,16 +267,9 @@
 
     def form(chunk, handed):
         if handed:
-            settle(inbox.at[chunk], in_recv.at[chunk + 1])
+            settle(inbox.at[chunk], in_recv.at[chunk])
         else:
-            @pl.when(chunk == 0)
-            def _():
-                for half in range(2):
-                    settle(inbox.at[0, pl.ds(0, n_mom - 1), half], in_recv.at[half])
-
-            @pl.when(chunk > 0)
-            def _():
-                settle(inbox.at[chunk, pl.ds(0, n_mom - 1)], in_recv.at[chunk + 1])
+            settle(inbox.at[chunk, pl.ds(0, n_mom - 1)], in_recv.at[chunk])
 
         for part, value in enumerate(pack(*(inbox[chunk, :, half].astype(jnp.float32) for half in range(2)))):
             wide[:, part * share:(part + 1) * share] = value
@@ -327,7 +293,7 @@
 
             if handed:
                 send(
-                    formed.at[chunk, mom], returned.at[chunks - 1, me], out_send.at[chunk], out_recv.at[chunks - 1],
+                    formed.at[chunk, mom], returned.at[HANDED, me], out_send.at[chunk], out_recv.at[HANDED],
                     mom, turn + ahead,
                 )
             else:
@@ -344,7 +310,7 @@
             returned[chunk, me] = formed[chunk, me]
 
     def finish(chunk):
-        given = last & (chunk == chunks - 1)
+        given = last & (chunk == HANDED)
 
         @pl.when(given)
         def _():
@@ -369,11 +335,11 @@
             lax.fori_loop(2 * step, 2 * step + 2, advance, 0)
             keep(step)
 
-        @pl.when((step >= 1) & ((step < chunks) | ((step == chunks) & jnp.logical_not(last))))
+        @pl.when((step >= 1) & (step < chunks + 1) & jnp.logical_not(last & (step - 1 == HANDED)))
         def _():
             form(step - 1, False)
 
-        @pl.when(step >= 2)
+        @pl.when((step >= 2) & jnp.logical_not(last & (step - 2 == HANDED)))
         def _():
             finish(step - 2)
 
@@ -384,6 +350,10 @@
     @pl.when(first)
     def _():
         form(chunks, True)
+
+    @pl.when(last)
+    def _():
+        finish(HANDED)
 
     def close_piece(piece, carry):
         @pl.when(core == 0)
@@ -408,20 +378,15 @@
             pair.wait_send()
 
     def close(chunk, carry):
-        given = last & (chunk == chunks - 1)
-
-        @pl.when(chunk == 0)
-        def _():
-            for half in range(2):
-                settle(outbox.at[0, pl.ds(0, n_mom - 1), half], in_send.at[half])
-
-        @pl.when((chunk > 0) & jnp.logical_not(given))
-        def _():
-            settle(outbox.at[chunk, pl.ds(0, n_mom - 1)], in_send.at[chunk + 1])
+        given = last & (chunk == HANDED)
+
+        @pl.when(jnp.logical_not(given))
+        def _():
+            settle(outbox.at[chunk, pl.ds(0, n_mom - 1)], in_send.at[chunk])
 
         @pl.when(given)
         def _():
-            settle(outbox.at[chunk], in_send.at[chunk + 1])
+            settle(outbox.at[chunk], in_send.at[chunk])
 
         @pl.when(jnp.logical_not(given))
         def _():
@@ -500,7 +465,7 @@
             pltpu.SemaphoreType.DMA((2,)),
             pltpu.SemaphoreType.DMA((2,)),
             twice, twice, twice, twice, twice,
-            *[pltpu.SemaphoreType.DMA((chunks + extra,)) for extra in (1, 2, 1, 0)],
+            *[pltpu.SemaphoreType.DMA((chunks + extra,)) for extra in (0, 1, 1, 0)],
         ],
         compiler_params=pltpu.CompilerParams(
             collective_id=0, has_side_effects=True, vmem_limit_bytes=58 << 20

time: 63.3 us -> 57.1 us (0.902)
  Pallas kernels: 62.5 us -> 56.3 us
    pallas_call x1, Pallas kernels: 60.1 us -> 53.9 us  [local(): pl.pallas_call(kernel, out_shape=(jax.ShapeDtypeStruct(source.shape, bf16...]
where the time goes in v7:
time: 57.1 us; the launch traced here: 56.9 us
  Pallas kernels  56.3 us (99%)
  between operations  0.64 us (1%)
    pallas_call x1, Pallas kernels, local(): pl.pallas_call(kernel, out_shape=(jax.ShapeDtypeStruct(source.shape, bf16...  53.9 us
    pallas_call x1, Pallas kernels, local(): pl.pallas_call(write_out, out_shape=[jax.ShapeDtypeStruct(result.shape, r...  2.39 us

profile of v7, /device:TPU:24, one launch (start us, length us, event | category | flops | bytes accessed | tf_op | source)
XLA Modules:
  0.0 56.9 jit_solution(16130664780464078669)
XLA Ops:
  0.6 53.9 %shard_map.86 = (bf16[2,1,256,512]{3,2,1,0:T(8,128)(2,1)}, f32[2,1,256,512]{3,2,1,0:T(8,128)}) custom-call(s32[3,8,32]{2,1,0:T(8,128)} %bitcast.2, s32[32]{0:T(128)} %counts_hbm.1, s32[8,32]{1,0:T(8,128)} %bitcast.3, f32[16]{0:T(128)} %vertex_hbm.1, f32[2,1,256,512]{3,2,1,0:T(8,128)} %source_hbm.1, f32[2,1,1,256,256]{4,3,2,1,0:T(8,128)} %inverse_hbm.1, ...), custom_call_target="tpu_custom_call" | custom-call | tf_op jit(solution)/shard_map/pallas_call | solution.py:435
  54.5 2.4 %shard_map.87 = (bf16[2,1,256,512]{3,2,1,0:T(8,128)(2,1)}, f32[2,1,256,512]{3,2,1,0:T(8,128)}) custom-call(bf16[2,1,256,512]{3,2,1,0:T(8,128)(2,1)} %get-tuple-element.4.solved, f32[2,1,256,512]{3,2,1,0:T(8,128)} %get-tuple-element.5.sigma), custom_call_target="tpu_custom_call" | custom-call | tf_op jit(solution)/shard_map/pallas_call | solution.py:478

commit v8 on v7

--- a/solution.py
+++ b/solution.py
@@ -325,35 +325,34 @@
         sigma[chunk, 1] = value[:, share:].reshape(rows, LANES)
         store(1, chunk).start()
 
-    def stage(step, carry):
-        @pl.when((core == 1) & (step < chunks))
-        def _():
-            compose(step)
-
-        @pl.when(step < chunks)
-        def _():
-            lax.fori_loop(2 * step, 2 * step + 2, advance, 0)
-            keep(step)
-
-        @pl.when((step >= 1) & (step < chunks + 1) & jnp.logical_not(last & (step - 1 == HANDED)))
-        def _():
-            form(step - 1, False)
-
-        @pl.when((step >= 2) & jnp.logical_not(last & (step - 2 == HANDED)))
-        def _():
-            finish(step - 2)
-
-        return carry
-
-    lax.fori_loop(0, chunks + 2, stage, 0)
+    def solve(chunk, carry):
+        @pl.when(core == 1)
+        def _():
+            compose(chunk)
+
+        lax.fori_loop(2 * chunk, 2 * chunk + 2, advance, 0)
+        keep(chunk)
+        return carry
+
+    def form_own(chunk, carry):
+        @pl.when(jnp.logical_not(last & (chunk == HANDED)))
+        def _():
+            form(chunk, False)
+
+        return carry
+
+    def finish_own(chunk, carry):
+        finish(chunk)
+        return carry
+
+    lax.fori_loop(0, chunks, solve, 0)
+    lax.fori_loop(0, chunks, form_own, 0)
 
     @pl.when(first)
     def _():
         form(chunks, True)
 
-    @pl.when(last)
-    def _():
-        finish(HANDED)
+    lax.fori_loop(0, chunks, finish_own, 0)
 
     def close_piece(piece, carry):
         @pl.when(core == 0)

time: 57.1 us -> 52.1 us (0.912)
  Pallas kernels: 56.3 us -> 51.3 us
    pallas_call x1, Pallas kernels: 53.9 us -> 49 us  [local(): pl.pallas_call(kernel, out_shape=(jax.ShapeDtypeStruct(source.shape, bf16...]
where the time goes in v8:
time: 52.1 us; the launch traced here: 52 us
  Pallas kernels  51.3 us (98%)
  between operations  0.64 us (1%)
    pallas_call x1, Pallas kernels, local(): pl.pallas_call(kernel, out_shape=(jax.ShapeDtypeStruct(source.shape, bf16...  49 us
    pallas_call x1, Pallas kernels, local(): pl.pallas_call(write_out, out_shape=[jax.ShapeDtypeStruct(result.shape, r...  2.39 us

profile of v8, /device:TPU:24, one launch (start us, length us, event | category | flops | bytes accessed | tf_op | source)
XLA Modules:
  0.0 52.0 jit_solution(477749116583969393)
XLA Ops:
  0.6 49.0 %shard_map.86 = (bf16[2,1,256,512]{3,2,1,0:T(8,128)(2,1)}, f32[2,1,256,512]{3,2,1,0:T(8,128)}) custom-call(s32[3,8,32]{2,1,0:T(8,128)} %bitcast.2, s32[32]{0:T(128)} %counts_hbm.1, s32[8,32]{1,0:T(8,128)} %bitcast.3, f32[16]{0:T(128)} %vertex_hbm.1, f32[2,1,256,512]{3,2,1,0:T(8,128)} %source_hbm.1, f32[2,1,1,256,256]{4,3,2,1,0:T(8,128)} %inverse_hbm.1, ...), custom_call_target="tpu_custom_call" | custom-call | tf_op jit(solution)/shard_map/pallas_call | solution.py:434
  49.6 2.4 %shard_map.87 = (bf16[2,1,256,512]{3,2,1,0:T(8,128)(2,1)}, f32[2,1,256,512]{3,2,1,0:T(8,128)}) custom-call(bf16[2,1,256,512]{3,2,1,0:T(8,128)(2,1)} %get-tuple-element.4.solved, f32[2,1,256,512]{3,2,1,0:T(8,128)} %get-tuple-element.5.sigma), custom_call_target="tpu_custom_call" | custom-call | tf_op jit(solution)/shard_map/pallas_call | solution.py:477

commit v9 on v8

--- a/solution.py
+++ b/solution.py
@@ -1,3 +1,5 @@
+import functools
+
 import jax
 import jax.numpy as jnp
 from jax import lax
@@ -7,7 +9,7 @@
 
 MESH = pl.DeviceIdType.MESH
 LANES = 128
-HANDED = 0
+HANDED = ((0, 0), (0, 1), (1, 0))
 
 
 def split(value):
@@ -69,8 +71,11 @@
     slots = moms.shape[1]
     core, plane, planes = lax.rem(turn, 2), turn // 2, n_tm // 2
     partner = turn + 1 - 2 * core
-    first, last = plane == 0, plane == planes - 1
-    ahead = 2 * (planes - 1)
+    first, behind = plane == 0, planes - 1 - plane
+
+    def is_handed(chunk):
+        return functools.reduce(jnp.logical_or, [(behind == back) & (chunk == which) for back, which in HANDED])
+
 
     loads = [
         pltpu.make_async_copy(here, there, load_sem.at[place])
@@ -238,25 +243,37 @@
 
         chunk, half = piece // 2, lax.rem(piece, 2)
         outbox[chunk, :, half] = greens[piece].reshape(n_mom, share, LANES).astype(jnp.bfloat16)
-        given = last & (chunk == HANDED)
+        given = is_handed(chunk)
 
         @pl.when(jnp.logical_not(given))
         def _():
             inbox[chunk, me, half] = outbox[chunk, me, half]
 
-        @pl.when(jnp.logical_not(given))
-        def _():
-            lax.fori_loop(1, n_mom, others(lambda other: send(
-                outbox.at[chunk, other, half], inbox.at[chunk, me, half], in_send.at[chunk], in_recv.at[chunk],
-                other, turn,
-            )), 0)
-
-        @pl.when(given)
-        def _():
-            lax.fori_loop(0, n_mom, others(lambda other: send(
-                outbox.at[chunk, other, half], inbox.at[chunks, me, half], in_send.at[chunk], in_recv.at[chunks],
-                other, lax.rem(turn + 2, n_tm),
-            )), 0)
+        def spread(part):
+            @pl.when(jnp.logical_not(given))
+            def _():
+                for step in range(1, n_mom):
+                    other = lax.rem(me + step, n_mom)
+                    send(
+                        outbox.at[(chunk, other, *part)], inbox.at[(chunk, me, *part)],
+                        in_send.at[chunk], in_recv.at[chunk], other, turn,
+                    )
+
+            @pl.when(given)
+            def _():
+                slot = chunks + 2 * behind + chunk
+                lax.fori_loop(0, n_mom, others(lambda other: send(
+                    outbox.at[(chunk, other, *part)], inbox.at[(slot, me, *part)],
+                    in_send.at[chunk], in_recv.at[slot], other, core,
+                )), 0)
+
+        @pl.when(chunk == 0)
+        def _():
+            spread((half,))
+
+        @pl.when((chunk > 0) & (half == 1))
+        def _():
+            spread(())
 
         return carry
 
@@ -293,8 +310,8 @@
 
             if handed:
                 send(
-                    formed.at[chunk, mom], returned.at[HANDED, me], out_send.at[chunk], out_recv.at[HANDED],
-                    mom, turn + ahead,
+                    formed.at[chunk, mom], returned.at[lax.rem(chunk - chunks, 2), me], out_send.at[chunk],
+                    out_recv.at[lax.rem(chunk - chunks, 2)], mom, turn + 2 * (planes - 1 - (chunk - chunks) // 2),
                 )
             else:
                 @pl.when(step < n_mom)
@@ -310,7 +327,7 @@
             returned[chunk, me] = formed[chunk, me]
 
     def finish(chunk):
-        given = last & (chunk == HANDED)
+        given = is_handed(chunk)
 
         @pl.when(given)
         def _():
@@ -326,7 +343,7 @@
         store(1, chunk).start()
 
     def solve(chunk, carry):
-        @pl.when(core == 1)
+        @pl.when((core == 1) & (chunk > plane))
         def _():
             compose(chunk)
 
@@ -335,7 +352,7 @@
         return carry
 
     def form_own(chunk, carry):
-        @pl.when(jnp.logical_not(last & (chunk == HANDED)))
+        @pl.when(jnp.logical_not(is_handed(chunk)))
         def _():
             form(chunk, False)
 
@@ -345,12 +362,24 @@
         finish(chunk)
         return carry
 
+    @pl.when(core == 1)
+    def _():
+        def compose_early(chunk, carry):
+            compose(chunk)
+            return carry
+
+        lax.fori_loop(0, lax.min(chunks, plane + 1), compose_early, 0)
+
     lax.fori_loop(0, chunks, solve, 0)
     lax.fori_loop(0, chunks, form_own, 0)
 
     @pl.when(first)
     def _():
-        form(chunks, True)
+        def form_other(place, carry):
+            form(chunks + lax.rem(place + len(HANDED) - 1, len(HANDED)), True)
+            return carry
+
+        lax.fori_loop(0, len(HANDED), form_other, 0)
 
     lax.fori_loop(0, chunks, finish_own, 0)
 
@@ -377,7 +406,7 @@
             pair.wait_send()
 
     def close(chunk, carry):
-        given = last & (chunk == HANDED)
+        given = is_handed(chunk)
 
         @pl.when(jnp.logical_not(given))
         def _():
@@ -399,7 +428,11 @@
 
     @pl.when(first)
     def _():
-        settle(formed.at[chunks], out_send.at[chunks])
+        def close_other(slot, carry):
+            settle(formed.at[slot], out_send.at[slot])
+            return carry
+
+        lax.fori_loop(chunks, chunks + len(HANDED), close_other, 0)
 
 
 def write_out(solved, sigma, solved_out, sigma_out, solved_held, sigma_held, in_sem, out_sem):
@@ -453,9 +486,9 @@
             pltpu.VMEM((2 * chunks, rows, LANES), f32),
             pltpu.VMEM((2 * chunks, rows, LANES), f32),
             pltpu.VMEM((chunks, n_mom, 2, share, LANES), bf16),
-            pltpu.VMEM((chunks + 1, n_mom, 2, share, LANES), bf16),
+            pltpu.VMEM((chunks + len(HANDED), n_mom, 2, share, LANES), bf16),
             pltpu.VMEM(piece[1:], f32),
-            pltpu.VMEM((chunks + 1, *piece[1:]), bf16),
+            pltpu.VMEM((chunks + len(HANDED), *piece[1:]), bf16),
             pltpu.VMEM(piece, bf16),
             pltpu.VMEM((chunks, 2, rows, LANES), bf16),
             pltpu.VMEM((chunks, 2, rows, LANES), f32),
@@ -464,7 +497,7 @@
             pltpu.SemaphoreType.DMA((2,)),
             pltpu.SemaphoreType.DMA((2,)),
             twice, twice, twice, twice, twice,
-            *[pltpu.SemaphoreType.DMA((chunks + extra,)) for extra in (0, 1, 1, 0)],
+            *[pltpu.SemaphoreType.DMA((chunks + extra,)) for extra in (0, len(HANDED), len(HANDED), 0)],
         ],
         compiler_params=pltpu.CompilerParams(
             collective_id=0, has_side_effects=True, vmem_limit_bytes=58 << 20

time: 52.1 us -> 53.7 us (1.031)
  Pallas kernels: 51.3 us -> 52.9 us
    pallas_call x1, Pallas kernels: 49 us -> 50.5 us  [local(): pl.pallas_call(kernel, out_shape=(jax.ShapeDtypeStruct(source.shape, bf16...]
where the time goes in v9:
time: 53.7 us; the launch traced here: 53.5 us
  Pallas kernels  52.9 us (99%)
  between operations  0.64 us (1%)
    pallas_call x1, Pallas kernels, local(): pl.pallas_call(kernel, out_shape=(jax.ShapeDtypeStruct(source.shape, bf16...  50.5 us
    pallas_call x1, Pallas kernels, local(): pl.pallas_call(write_out, out_shape=[jax.ShapeDtypeStruct(result.shape, r...  2.39 us

profile of v9, /device:TPU:24, one launch (start us, length us, event | category | flops | bytes accessed | tf_op | source)
XLA Modules:
  0.0 53.5 jit_solution(8373806762374517185)
XLA Ops:
  0.6 50.5 %shard_map.86 = (bf16[2,1,256,512]{3,2,1,0:T(8,128)(2,1)}, f32[2,1,256,512]{3,2,1,0:T(8,128)}) custom-call(s32[3,8,32]{2,1,0:T(8,128)} %bitcast.2, s32[32]{0:T(128)} %counts_hbm.1, s32[8,32]{1,0:T(8,128)} %bitcast.3, f32[16]{0:T(128)} %vertex_hbm.1, f32[2,1,256,512]{3,2,1,0:T(8,128)} %source_hbm.1, f32[2,1,1,256,256]{4,3,2,1,0:T(8,128)} %inverse_hbm.1, ...), custom_call_target="tpu_custom_call" | custom-call | tf_op jit(solution)/shard_map/pallas_call | solution.py:467
  51.1 2.4 %shard_map.87 = (bf16[2,1,256,512]{3,2,1,0:T(8,128)(2,1)}, f32[2,1,256,512]{3,2,1,0:T(8,128)}) custom-call(bf16[2,1,256,512]{3,2,1,0:T(8,128)(2,1)} %get-tuple-element.4.solved, f32[2,1,256,512]{3,2,1,0:T(8,128)} %get-tuple-element.5.sigma), custom_call_target="tpu_custom_call" | custom-call | tf_op jit(solution)/shard_map/pallas_call | solution.py:510

commit v10 on v9

--- a/solution.py
+++ b/solution.py
@@ -9,6 +9,7 @@
 
 MESH = pl.DeviceIdType.MESH
 LANES = 128
+EXTRA = 16
 HANDED = ((0, 0), (0, 1), (1, 0))
 
 
@@ -56,11 +57,25 @@
     return blocks
 
 
+def encode(value):
+    peak = jnp.max(jnp.abs(value), axis=0, keepdims=True)
+    level = jnp.ceil(jnp.log2(jnp.maximum(peak * 1.0001, 1e-30)))
+    levels = jnp.broadcast_to(level, (EXTRA, value.shape[1]))
+    code = jnp.concatenate([jnp.round(value * jnp.exp2(15.0 - level)), levels], axis=0)
+    return code.astype(jnp.int32).astype(jnp.int16)
+
+
+def decode(code):
+    value = code.astype(jnp.int32).astype(jnp.float32)
+    rows = code.shape[0] - EXTRA
+    return value[:rows] * jnp.exp2(value[rows:rows + 1] - 15.0)
+
+
 def kernel(
     moms_hbm, counts_hbm, weights_hbm, vertex_hbm, source_hbm, inverse_hbm, coupling_hbm,
     solved_hbm, sigma_hbm,
     moms, counts, weights, vertex, source, inverse, coupling, left_high, left_low, own_high, own_low, pair_high, pair_low, step_high, step_low,
-    driven, lent, entering, greens,
+    driven, lent, wire, entering, greens,
     outbox, inbox, wide, formed, returned, solved, sigma,
     load_sem, store_sem, pair_send, pair_recv, lend_send, lend_recv, pass_send, hop_send, hop_recv, in_send, in_recv, out_send, out_recv,
 ):
@@ -147,7 +162,7 @@
 
     def hop(piece):
         return to(
-            lax.rem(turn + 2, n_tm), greens.at[piece], entering.at[piece], hop_send.at[piece], hop_recv.at[piece]
+            lax.rem(turn + 2, n_tm), wire.at[piece], entering.at[piece], hop_send.at[piece], hop_recv.at[piece]
         )
 
     def forward(piece):
@@ -177,6 +192,14 @@
             return carry
 
         lax.fori_loop(1, chunks, drive_and_lend, 0)
+
+    @pl.when(core == 1)
+    def _():
+        def drive_rest(chunk, carry):
+            drive(chunk)
+            return carry
+
+        lax.fori_loop(1, chunks, drive_rest, 0)
 
     @pl.when((core == 1) & (plane > 0))
     def _():
@@ -190,10 +213,6 @@
         keep_matrix(step_high, step_low, join(both))
 
     def compose(chunk):
-        @pl.when(chunk > 0)
-        def _():
-            drive(chunk)
-
         for half in range(2):
             lend(2 * chunk + half).wait_recv()
         value = jnp.concatenate([lent[2 * chunk], lent[2 * chunk + 1]], axis=1)
@@ -234,11 +253,12 @@
             def _():
                 forward(piece).start()
 
-            [block] = packed_times(step_high[...], step_low[...], entering[piece])
+            [block] = packed_times(step_high[...], step_low[...], decode(entering[piece]))
             greens[piece] = driven[piece] + block
 
         @pl.when((core == 1) & (plane < planes - 1))
         def _():
+            wire[piece] = encode(greens[piece])
             hop(piece).start()
 
         chunk, half = piece // 2, lax.rem(piece, 2)
@@ -483,7 +503,8 @@
             *[pltpu.VMEM((2 * rows, rows), bf16) for _ in range(8)],
             pltpu.VMEM((2 * chunks, rows, LANES), f32),
             pltpu.VMEM((2 * chunks, rows, LANES), f32),
-            pltpu.VMEM((2 * chunks, rows, LANES), f32),
+            pltpu.VMEM((2 * chunks, rows + EXTRA, LANES), jnp.int16),
+            pltpu.VMEM((2 * chunks, rows + EXTRA, LANES), jnp.int16),
             pltpu.VMEM((2 * chunks, rows, LANES), f32),
             pltpu.VMEM((chunks, n_mom, 2, share, LANES), bf16),
             pltpu.VMEM((chunks + len(HANDED), n_mom, 2, share, LANES), bf16),

time: 53.7 us -> 50 us (0.931)
  Pallas kernels: 52.9 us -> 49.1 us
    pallas_call x1, Pallas kernels: 50.5 us -> 46.8 us  [local(): pl.pallas_call(kernel, out_shape=(jax.ShapeDtypeStruct(source.shape, bf16...]
where the time goes in v10:
time: 50 us; the launch traced here: 49.8 us
  Pallas kernels  49.1 us (98%)
  between operations  0.64 us (1%)
    pallas_call x1, Pallas kernels, local(): pl.pallas_call(kernel, out_shape=(jax.ShapeDtypeStruct(source.shape, bf16...  46.8 us
    pallas_call x1, Pallas kernels, local(): pl.pallas_call(write_out, out_shape=[jax.ShapeDtypeStruct(result.shape, r...  2.39 us

profile of v10, /device:TPU:24, one launch (start us, length us, event | category | flops | bytes accessed | tf_op | source)
XLA Modules:
  0.0 49.8 jit_solution(5424525871837297876)
XLA Ops:
  0.6 46.8 %shard_map.86 = (bf16[2,1,256,512]{3,2,1,0:T(8,128)(2,1)}, f32[2,1,256,512]{3,2,1,0:T(8,128)}) custom-call(s32[3,8,32]{2,1,0:T(8,128)} %bitcast.2, s32[32]{0:T(128)} %counts_hbm.1, s32[8,32]{1,0:T(8,128)} %bitcast.3, f32[16]{0:T(128)} %vertex_hbm.1, f32[2,1,256,512]{3,2,1,0:T(8,128)} %source_hbm.1, f32[2,1,1,256,256]{4,3,2,1,0:T(8,128)} %inverse_hbm.1, ...), custom_call_target="tpu_custom_call" | custom-call | tf_op jit(solution)/shard_map/pallas_call | solution.py:487
  47.4 2.4 %shard_map.87 = (bf16[2,1,256,512]{3,2,1,0:T(8,128)(2,1)}, f32[2,1,256,512]{3,2,1,0:T(8,128)}) custom-call(bf16[2,1,256,512]{3,2,1,0:T(8,128)(2,1)} %get-tuple-element.4.solved, f32[2,1,256,512]{3,2,1,0:T(8,128)} %get-tuple-element.5.sigma), custom_call_target="tpu_custom_call" | custom-call | tf_op jit(solution)/shard_map/pallas_call | solution.py:531

commit v11 on v10

--- a/solution.py
+++ b/solution.py
@@ -1,5 +1,3 @@
-import functools
-
 import jax
 import jax.numpy as jnp
 from jax import lax
@@ -10,7 +8,7 @@
 MESH = pl.DeviceIdType.MESH
 LANES = 128
 EXTRA = 16
-HANDED = ((0, 0), (0, 1), (1, 0))
+HANDED = 2
 
 
 def split(value):
@@ -73,15 +71,15 @@
 
 def kernel(
     moms_hbm, counts_hbm, weights_hbm, vertex_hbm, source_hbm, inverse_hbm, coupling_hbm,
-    solved_hbm, sigma_hbm,
+    solved_out, sigma_out,
     moms, counts, weights, vertex, source, inverse, coupling, left_high, left_low, own_high, own_low, pair_high, pair_low, step_high, step_low,
     driven, lent, wire, entering, greens,
-    outbox, inbox, wide, formed, returned, solved, sigma,
-    load_sem, store_sem, pair_send, pair_recv, lend_send, lend_recv, pass_send, hop_send, hop_recv, in_send, in_recv, out_send, out_recv,
+    outbox, inbox, wide, formed, returned,
+    load_sem, pair_send, pair_recv, lend_send, lend_recv, pass_send, hop_send, hop_recv, in_send, in_recv, out_send, out_recv,
 ):
     n_mom, n_tm = lax.axis_size("mom"), lax.axis_size("tm")
     me, turn = lax.axis_index("mom"), lax.axis_index("tm")
-    rows, chunks = sigma.shape[2], sigma.shape[0]
+    rows, chunks = driven.shape[1], driven.shape[0] // 2
     share = rows // n_mom
     slots = moms.shape[1]
     core, plane, planes = lax.rem(turn, 2), turn // 2, n_tm // 2
@@ -89,7 +87,7 @@
     first, behind = plane == 0, planes - 1 - plane
 
     def is_handed(chunk):
-        return functools.reduce(jnp.logical_or, [(behind == back) & (chunk == which) for back, which in HANDED])
+        return (behind < HANDED) & (chunk == 0)
 
 
     loads = [
@@ -235,10 +233,8 @@
 
         return one
 
-    def store(which, chunk):
-        here, there = ((solved, solved_hbm), (sigma, sigma_hbm))[which]
-        columns = pl.ds(pl.multiple_of(chunk * LANES, LANES), LANES)
-        return pltpu.make_async_copy(here.at[chunk], there.at[:, 0, :, columns], store_sem.at[which, chunk])
+    def span(chunk):
+        return pl.ds(pl.multiple_of(chunk * LANES, LANES), LANES)
 
     def advance(piece, carry):
         @pl.when(plane == 0)
@@ -281,7 +277,7 @@
 
             @pl.when(given)
             def _():
-                slot = chunks + 2 * behind + chunk
+                slot = chunks + behind
                 lax.fori_loop(0, n_mom, others(lambda other: send(
                     outbox.at[(chunk, other, *part)], inbox.at[(slot, me, *part)],
                     in_send.at[chunk], in_recv.at[slot], other, core,
@@ -299,8 +295,7 @@
 
     def keep(chunk):
         for part, value in enumerate(pack(greens[2 * chunk], greens[2 * chunk + 1])):
-            solved[chunk, part] = value.astype(jnp.bfloat16)
-        store(0, chunk).start()
+            solved_out[part, :, span(chunk)] = value.astype(jnp.bfloat16)
 
     def form(chunk, handed):
         if handed:
@@ -330,8 +325,8 @@
 
             if handed:
                 send(
-                    formed.at[chunk, mom], returned.at[lax.rem(chunk - chunks, 2), me], out_send.at[chunk],
-                    out_recv.at[lax.rem(chunk - chunks, 2)], mom, turn + 2 * (planes - 1 - (chunk - chunks) // 2),
+                    formed.at[chunk, mom], returned.at[0, me], out_send.at[chunk],
+                    out_recv.at[0], mom, turn + 2 * (planes - 1 - (chunk - chunks)),
                 )
             else:
                 @pl.when(step < n_mom)
@@ -358,9 +353,8 @@
             settle(returned.at[chunk, pl.ds(0, n_mom - 1)], out_recv.at[chunk])
 
         value = returned[chunk].astype(jnp.float32)
-        sigma[chunk, 0] = value[:, :share].reshape(rows, LANES)
-        sigma[chunk, 1] = value[:, share:].reshape(rows, LANES)
-        store(1, chunk).start()
+        sigma_out[0, :, span(chunk)] = value[:, :share].reshape(rows, LANES)
+        sigma_out[1, :, span(chunk)] = value[:, share:].reshape(rows, LANES)
 
     def solve(chunk, carry):
         @pl.when((core == 1) & (chunk > plane))
@@ -379,7 +373,7 @@
         return carry
 
     def finish_own(chunk, carry):
-        finish(chunk)
+        finish(lax.rem(chunk + plane // (planes - HANDED), chunks))
         return carry
 
     @pl.when(core == 1)
@@ -396,10 +390,10 @@
     @pl.when(first)
     def _():
         def form_other(place, carry):
-            form(chunks + lax.rem(place + len(HANDED) - 1, len(HANDED)), True)
-            return carry
-
-        lax.fori_loop(0, len(HANDED), form_other, 0)
+            form(chunks + HANDED - 1 - place, True)
+            return carry
+
+        lax.fori_loop(0, HANDED, form_other, 0)
 
     lax.fori_loop(0, chunks, finish_own, 0)
 
@@ -439,9 +433,6 @@
         @pl.when(jnp.logical_not(given))
         def _():
             settle(formed.at[chunk, pl.ds(0, n_mom - 1)], out_send.at[chunk])
-
-        store(0, chunk).wait()
-        store(1, chunk).wait()
         return carry
 
     lax.fori_loop(0, chunks, close, 0)
@@ -452,28 +443,22 @@
             settle(formed.at[slot], out_send.at[slot])
             return carry
 
-        lax.fori_loop(chunks, chunks + len(HANDED), close_other, 0)
-
-
-def write_out(solved, sigma, solved_out, sigma_out, solved_held, sigma_held, in_sem, out_sem):
-    blocks = in_sem.shape[2]
-    height = solved_held.shape[1] // blocks
-    moves = []
-    for place, (src, held, dst) in enumerate(((sigma, sigma_held, sigma_out), (solved, solved_held, solved_out))):
+        lax.fori_loop(chunks, chunks + HANDED, close_other, 0)
+
+
+def write_out(solved, sigma, solved_out, sigma_out, sem):
+    blocks = sem.shape[2]
+    height = solved.shape[1] // blocks
+    copies = []
+    for place, (src, dst) in enumerate(((sigma, sigma_out), (solved, solved_out))):
         for part in range(2):
             for block in range(blocks):
                 span = pl.ds(block * height, height)
-                moves.append((
-                    pltpu.make_async_copy(src.at[part, 0, span], held.at[part, span], in_sem.at[place, part, block]),
-                    pltpu.make_async_copy(held.at[part, span], dst.at[part, 0, span], out_sem.at[place, part, block]),
-                ))
-    for arrive, _ in moves:
-        arrive.start()
-    for arrive, leave in moves:
-        arrive.wait()
-        leave.start()
-    for _, leave in moves:
-        leave.wait()
+                copies.append(pltpu.make_async_copy(src.at[part, span], dst.at[part, 0, span], sem.at[place, part, block]))
+    for copy in copies:
+        copy.start()
+    for copy in copies:
+        copy.wait()
 
 
 def local(source, inverse_diag, coupling, pair_moms, pair_count, pair_weight, vertex):
@@ -481,17 +466,17 @@
     n_mom = lax.axis_size("mom")
     chunks, share = columns // LANES, rows // n_mom
     f32, bf16 = jnp.float32, jnp.bfloat16
-    hbm = pl.BlockSpec(memory_space=pltpu.HBM)
+    hbm, vmem = pl.BlockSpec(memory_space=pltpu.HBM), pl.BlockSpec(memory_space=pltpu.VMEM)
     piece = (chunks, n_mom, 2 * share, LANES)
     twice = pltpu.SemaphoreType.DMA((2 * chunks,))
     results = pl.pallas_call(
         kernel,
         out_shape=(
-            jax.ShapeDtypeStruct(source.shape, bf16),
-            jax.ShapeDtypeStruct(source.shape, f32),
+            pltpu.VMEM((2, rows, columns), bf16),
+            pltpu.VMEM((2, rows, columns), f32),
         ),
         in_specs=[hbm] * 7,
-        out_specs=(hbm, hbm),
+        out_specs=(vmem, vmem),
         scratch_shapes=[
             pltpu.SMEM(pair_moms.shape[::-1], jnp.int32),
             pltpu.SMEM(pair_count.shape, jnp.int32),
@@ -507,18 +492,15 @@
             pltpu.VMEM((2 * chunks, rows + EXTRA, LANES), jnp.int16),
             pltpu.VMEM((2 * chunks, rows, LANES), f32),
             pltpu.VMEM((chunks, n_mom, 2, share, LANES), bf16),
-            pltpu.VMEM((chunks + len(HANDED), n_mom, 2, share, LANES), bf16),
+            pltpu.VMEM((chunks + HANDED, n_mom, 2, share, LANES), bf16),
             pltpu.VMEM(piece[1:], f32),
-            pltpu.VMEM((chunks + len(HANDED), *piece[1:]), bf16),
+            pltpu.VMEM((chunks + HANDED, *piece[1:]), bf16),
             pltpu.VMEM(piece, bf16),
-            pltpu.VMEM((chunks, 2, rows, LANES), bf16),
-            pltpu.VMEM((chunks, 2, rows, LANES), f32),
             pltpu.SemaphoreType.DMA((7,)),
-            pltpu.SemaphoreType.DMA((2, chunks)),
             pltpu.SemaphoreType.DMA((2,)),
             pltpu.SemaphoreType.DMA((2,)),
             twice, twice, twice, twice, twice,
-            *[pltpu.SemaphoreType.DMA((chunks + extra,)) for extra in (0, len(HANDED), len(HANDED), 0)],
+            *[pltpu.SemaphoreType.DMA((chunks + extra,)) for extra in (0, HANDED, HANDED, 0)],
         ],
         compiler_params=pltpu.CompilerParams(
             collective_id=0, has_side_effects=True, vmem_limit_bytes=58 << 20
@@ -527,18 +509,13 @@
         jnp.transpose(pair_moms, (2, 1, 0)), pair_count, jnp.transpose(pair_weight, (1, 0)), vertex,
         source, inverse_diag, coupling,
     )
-    blocks = 4
     return pl.pallas_call(
         write_out,
-        out_shape=[jax.ShapeDtypeStruct(result.shape, result.dtype) for result in results],
-        in_specs=[hbm] * 2,
-        out_specs=(hbm, hbm),
-        scratch_shapes=[
-            pltpu.VMEM((2, rows, columns), bf16),
-            pltpu.VMEM((2, rows, columns), f32),
-            pltpu.SemaphoreType.DMA((2, 2, blocks)),
-            pltpu.SemaphoreType.DMA((2, 2, blocks)),
-        ],
+        out_shape=[jax.ShapeDtypeStruct(source.shape, dtype) for dtype in (bf16, f32)],
+        in_specs=[vmem] * 2,
+        out_specs=[hbm] * 2,
+        scratch_shapes=[pltpu.SemaphoreType.DMA((2, 2, 4))],
+        compiler_params=pltpu.CompilerParams(vmem_limit_bytes=32 << 20),
     )(*results)
 
 

time: 50 us -> 48.2 us (0.964)
  Pallas kernels: 49.1 us -> 47.4 us
    pallas_call x2, Pallas kernels: 49.1 us -> 47.4 us  [the longest x1 46.2 us: local(): pl.pallas_call(kernel, out_shape=(pltpu.VMEM((2, rows, columns), bf16), p...]
where the time goes in v11:
time: 48.2 us; the launch traced here: 48.1 us
  Pallas kernels  47.4 us (98%)
  between operations  0.64 us (1%)
    pallas_call x1, Pallas kernels, local(): pl.pallas_call(kernel, out_shape=(pltpu.VMEM((2, rows, columns), bf16), p...  46.2 us
    pallas_call x1, Pallas kernels, local(): pl.pallas_call(write_out, out_shape=[jax.ShapeDtypeStruct(source.shape, d...  1.26 us

profile of v11, /device:TPU:24, one launch (start us, length us, event | category | flops | bytes accessed | tf_op | source)
XLA Modules:
  0.0 48.1 jit_solution(12000097316311337026)
XLA Ops:
  0.6 46.2 %shard_map.86 = (bf16[2,256,512]{2,1,0:T(8,128)(2,1)S(1)}, f32[2,256,512]{2,1,0:T(8,128)S(1)}) custom-call(s32[3,8,32]{2,1,0:T(8,128)} %bitcast.2, s32[32]{0:T(128)} %counts_hbm.1, s32[8,32]{1,0:T(8,128)} %bitcast.3, f32[16]{0:T(128)} %vertex_hbm.1, f32[2,1,256,512]{3,2,1,0:T(8,128)} %source_hbm.1, f32[2,1,1,256,256]{4,3,2,1,0:T(8,128)} %inverse_hbm.1, ...), custom_call_target="tpu_custom_call" | custom-call | tf_op jit(solution)/shard_map/pallas_call | solution.py:472
  46.8 1.3 %shard_map.87 = (bf16[2,1,256,512]{3,2,1,0:T(8,128)(2,1)}, f32[2,1,256,512]{3,2,1,0:T(8,128)}) custom-call(bf16[2,256,512]{2,1,0:T(8,128)(2,1)S(1)} %get-tuple-element.4.solved, f32[2,256,512]{2,1,0:T(8,128)S(1)} %get-tuple-element.5.sigma), custom_call_target="tpu_custom_call" | custom-call | tf_op jit(solution)/shard_map/pallas_call | solution.py:512

commit v12 on v11

--- a/solution.py
+++ b/solution.py
@@ -8,7 +8,7 @@
 MESH = pl.DeviceIdType.MESH
 LANES = 128
 EXTRA = 16
-HANDED = 2
+HANDED = 3
 
 
 def split(value):
@@ -87,7 +87,14 @@
     first, behind = plane == 0, planes - 1 - plane
 
     def is_handed(chunk):
-        return (behind < HANDED) & (chunk == 0)
+        from_last = (behind == 0) & ((chunk == 0) | ((chunk == 1) & (core == 0)))
+        return from_last | ((behind == 1) & (chunk == chunks // 2))
+
+    def handed_from(slot):
+        return lax.rem(slot, 2), slot // 2 + lax.rem(slot, 2) * (chunks // 2)
+
+    def slot_of(chunk):
+        return chunks + behind + 2 * chunk * (1 - behind)
 
 
     loads = [
@@ -277,7 +284,7 @@
 
             @pl.when(given)
             def _():
-                slot = chunks + behind
+                slot = slot_of(chunk)
                 lax.fori_loop(0, n_mom, others(lambda other: send(
                     outbox.at[(chunk, other, *part)], inbox.at[(slot, me, *part)],
                     in_send.at[chunk], in_recv.at[slot], other, core,
@@ -324,9 +331,10 @@
             formed[chunk, mom] = jnp.concatenate([total_real, total_imag], axis=0).astype(jnp.bfloat16)
 
             if handed:
+                back, which = handed_from(chunk - chunks)
                 send(
-                    formed.at[chunk, mom], returned.at[0, me], out_send.at[chunk],
-                    out_recv.at[0], mom, turn + 2 * (planes - 1 - (chunk - chunks)),
+                    formed.at[chunk, mom], returned.at[which, me], out_send.at[chunk],
+                    out_recv.at[which], mom, turn + 2 * (planes - 1 - back),
                 )
             else:
                 @pl.when(step < n_mom)
@@ -373,7 +381,7 @@
         return carry
 
     def finish_own(chunk, carry):
-        finish(lax.rem(chunk + plane // (planes - HANDED), chunks))
+        finish(lax.rem(chunk + (2 * plane // planes) * (2 + behind), chunks))
         return carry
 
     @pl.when(core == 1)
@@ -390,10 +398,10 @@
     @pl.when(first)
     def _():
         def form_other(place, carry):
-            form(chunks + HANDED - 1 - place, True)
-            return carry
-
-        lax.fori_loop(0, HANDED, form_other, 0)
+            form(chunks + place, True)
+            return carry
+
+        lax.fori_loop(0, HANDED - core, form_other, 0)
 
     lax.fori_loop(0, chunks, finish_own, 0)
 
@@ -443,7 +451,7 @@
             settle(formed.at[slot], out_send.at[slot])
             return carry
 
-        lax.fori_loop(chunks, chunks + HANDED, close_other, 0)
+        lax.fori_loop(chunks, chunks + HANDED - core, close_other, 0)
 
 
 def write_out(solved, sigma, solved_out, sigma_out, sem):

time: 48.2 us -> 47.5 us (0.985)
  Pallas kernels: 47.4 us -> 46.7 us
    pallas_call x1, Pallas kernels: 46.2 us -> 45.4 us  [local(): pl.pallas_call(kernel, out_shape=(pltpu.VMEM((2, rows, columns), bf16), p...]
where the time goes in v12:
time: 47.5 us; the launch traced here: 47.4 us
  Pallas kernels  46.7 us (98%)
  between operations  0.64 us (1%)
    pallas_call x1, Pallas kernels, local(): pl.pallas_call(kernel, out_shape=(pltpu.VMEM((2, rows, columns), bf16), p...  45.4 us
    pallas_call x1, Pallas kernels, local(): pl.pallas_call(write_out, out_shape=[jax.ShapeDtypeStruct(source.shape, d...  1.26 us

profile of v12, /device:TPU:24, one launch (start us, length us, event | category | flops | bytes accessed | tf_op | source)
XLA Modules:
  0.0 47.4 jit_solution(11272469582599249210)
XLA Ops:
  0.6 45.4 %shard_map.86 = (bf16[2,256,512]{2,1,0:T(8,128)(2,1)S(1)}, f32[2,256,512]{2,1,0:T(8,128)S(1)}) custom-call(s32[3,8,32]{2,1,0:T(8,128)} %bitcast.2, s32[32]{0:T(128)} %counts_hbm.1, s32[8,32]{1,0:T(8,128)} %bitcast.3, f32[16]{0:T(128)} %vertex_hbm.1, f32[2,1,256,512]{3,2,1,0:T(8,128)} %source_hbm.1, f32[2,1,1,256,256]{4,3,2,1,0:T(8,128)} %inverse_hbm.1, ...), custom_call_target="tpu_custom_call" | custom-call | tf_op jit(solution)/shard_map/pallas_call | solution.py:480
  46.1 1.3 %shard_map.87 = (bf16[2,1,256,512]{3,2,1,0:T(8,128)(2,1)}, f32[2,1,256,512]{3,2,1,0:T(8,128)}) custom-call(bf16[2,256,512]{2,1,0:T(8,128)(2,1)S(1)} %get-tuple-element.4.solved, f32[2,256,512]{2,1,0:T(8,128)S(1)} %get-tuple-element.5.sigma), custom_call_target="tpu_custom_call" | custom-call | tf_op jit(solution)/shard_map/pallas_call | solution.py:520

commit v13 on v12

--- a/solution.py
+++ b/solution.py
@@ -8,6 +8,7 @@
 MESH = pl.DeviceIdType.MESH
 LANES = 128
 EXTRA = 16
+EARLY = 2
 HANDED = 3
 
 
@@ -87,11 +88,11 @@
     first, behind = plane == 0, planes - 1 - plane
 
     def is_handed(chunk):
-        from_last = (behind == 0) & ((chunk == 0) | ((chunk == 1) & (core == 0)))
-        return from_last | ((behind == 1) & (chunk == chunks // 2))
+        from_last = (behind == 0) & (chunk < 2)
+        return from_last | ((behind == 1) & (chunk == 1))
 
     def handed_from(slot):
-        return lax.rem(slot, 2), slot // 2 + lax.rem(slot, 2) * (chunks // 2)
+        return lax.rem(slot, 2), slot // 2 + lax.rem(slot, 2)
 
     def slot_of(chunk):
         return chunks + behind + 2 * chunk * (1 - behind)
@@ -290,14 +291,7 @@
                     in_send.at[chunk], in_recv.at[slot], other, core,
                 )), 0)
 
-        @pl.when(chunk == 0)
-        def _():
-            spread((half,))
-
-        @pl.when((chunk > 0) & (half == 1))
-        def _():
-            spread(())
-
+        spread((half,))
         return carry
 
     def keep(chunk):
@@ -381,7 +375,7 @@
         return carry
 
     def finish_own(chunk, carry):
-        finish(lax.rem(chunk + (2 * plane // planes) * (2 + behind), chunks))
+        finish(lax.rem(chunk + (2 * plane // planes) * 2, chunks))
         return carry
 
     @pl.when(core == 1)
@@ -393,7 +387,7 @@
         lax.fori_loop(0, lax.min(chunks, plane + 1), compose_early, 0)
 
     lax.fori_loop(0, chunks, solve, 0)
-    lax.fori_loop(0, chunks, form_own, 0)
+    lax.fori_loop(0, EARLY, form_own, 0)
 
     @pl.when(first)
     def _():
@@ -401,8 +395,9 @@
             form(chunks + place, True)
             return carry
 
-        lax.fori_loop(0, HANDED - core, form_other, 0)
-
+        lax.fori_loop(0, HANDED, form_other, 0)
+
+    lax.fori_loop(EARLY, chunks, form_own, 0)
     lax.fori_loop(0, chunks, finish_own, 0)
 
     def close_piece(piece, carry):
@@ -451,7 +446,7 @@
             settle(formed.at[slot], out_send.at[slot])
             return carry
 
-        lax.fori_loop(chunks, chunks + HANDED - core, close_other, 0)
+        lax.fori_loop(chunks, chunks + HANDED, close_other, 0)
 
 
 def write_out(solved, sigma, solved_out, sigma_out, sem):

time: 47.5 us -> 50.9 us (1.072)
  the two profiles are of different devices: /device:TPU:24 before, /device:TPU:2 now
where the time goes in v13:
time: 50.9 us; the launch traced here: 50.8 us
  Pallas kernels  50.2 us (99%)
  between operations  0.64 us (1%)
    pallas_call x1, Pallas kernels, local(): pl.pallas_call(kernel, out_shape=(pltpu.VMEM((2, rows, columns), bf16), p...  48.9 us
    pallas_call x1, Pallas kernels, local(): pl.pallas_call(write_out, out_shape=[jax.ShapeDtypeStruct(source.shape, d...  1.26 us

profile of v13, /device:TPU:2, one launch (start us, length us, event | category | flops | bytes accessed | tf_op | source)
XLA Modules:
  0.0 50.8 jit_solution(3800969062965029449)
XLA Ops:
  0.6 48.9 %shard_map.86 = (bf16[2,256,512]{2,1,0:T(8,128)(2,1)S(1)}, f32[2,256,512]{2,1,0:T(8,128)S(1)}) custom-call(s32[3,8,32]{2,1,0:T(8,128)} %bitcast.2, s32[32]{0:T(128)} %counts_hbm.1, s32[8,32]{1,0:T(8,128)} %bitcast.3, f32[16]{0:T(128)} %vertex_hbm.1, f32[2,1,256,512]{3,2,1,0:T(8,128)} %source_hbm.1, f32[2,1,1,256,256]{4,3,2,1,0:T(8,128)} %inverse_hbm.1, ...), custom_call_target="tpu_custom_call" | custom-call | tf_op jit(solution)/shard_map/pallas_call | solution.py:475
  49.5 1.3 %shard_map.87 = (bf16[2,1,256,512]{3,2,1,0:T(8,128)(2,1)}, f32[2,1,256,512]{3,2,1,0:T(8,128)}) custom-call(bf16[2,256,512]{2,1,0:T(8,128)(2,1)S(1)} %get-tuple-element.4.solved, f32[2,256,512]{2,1,0:T(8,128)S(1)} %get-tuple-element.5.sigma), custom_call_target="tpu_custom_call" | custom-call | tf_op jit(solution)/shard_map/pallas_call | solution.py:515

commit v14 on v13

--- a/solution.py
+++ b/solution.py
@@ -8,8 +8,7 @@
 MESH = pl.DeviceIdType.MESH
 LANES = 128
 EXTRA = 16
-EARLY = 2
-HANDED = 3
+HANDED = 2
 
 
 def split(value):
@@ -88,7 +87,7 @@
     first, behind = plane == 0, planes - 1 - plane
 
     def is_handed(chunk):
-        from_last = (behind == 0) & (chunk < 2)
+        from_last = (behind == 0) & (chunk == 0)
         return from_last | ((behind == 1) & (chunk == 1))
 
     def handed_from(slot):
@@ -387,7 +386,7 @@
         lax.fori_loop(0, lax.min(chunks, plane + 1), compose_early, 0)
 
     lax.fori_loop(0, chunks, solve, 0)
-    lax.fori_loop(0, EARLY, form_own, 0)
+    lax.fori_loop(0, chunks, form_own, 0)
 
     @pl.when(first)
     def _():
@@ -397,7 +396,6 @@
 
         lax.fori_loop(0, HANDED, form_other, 0)
 
-    lax.fori_loop(EARLY, chunks, form_own, 0)
     lax.fori_loop(0, chunks, finish_own, 0)
 
     def close_piece(piece, carry):

time: 50.9 us -> 46.5 us (0.914)
  the two profiles are of different devices: /device:TPU:2 before, /device:TPU:24 now
where the time goes in v14:
time: 46.5 us; the launch traced here: 46.4 us
  Pallas kernels  45.8 us (98%)
  between operations  0.64 us (1%)
    pallas_call x1, Pallas kernels, local(): pl.pallas_call(kernel, out_shape=(pltpu.VMEM((2, rows, columns), bf16), p...  44.5 us
    pallas_call x1, Pallas kernels, local(): pl.pallas_call(write_out, out_shape=[jax.ShapeDtypeStruct(source.shape, d...  1.26 us

profile of v14, /device:TPU:24, one launch (start us, length us, event | category | flops | bytes accessed | tf_op | source)
XLA Modules:
  0.0 46.4 jit_solution(313536305665403110)
XLA Ops:
  0.6 44.5 %shard_map.86 = (bf16[2,256,512]{2,1,0:T(8,128)(2,1)S(1)}, f32[2,256,512]{2,1,0:T(8,128)S(1)}) custom-call(s32[3,8,32]{2,1,0:T(8,128)} %bitcast.2, s32[32]{0:T(128)} %counts_hbm.1, s32[8,32]{1,0:T(8,128)} %bitcast.3, f32[16]{0:T(128)} %vertex_hbm.1, f32[2,1,256,512]{3,2,1,0:T(8,128)} %source_hbm.1, f32[2,1,1,256,256]{4,3,2,1,0:T(8,128)} %inverse_hbm.1, ...), custom_call_target="tpu_custom_call" | custom-call | tf_op jit(solution)/shard_map/pallas_call | solution.py:473
  45.2 1.3 %shard_map.87 = (bf16[2,1,256,512]{3,2,1,0:T(8,128)(2,1)}, f32[2,1,256,512]{3,2,1,0:T(8,128)}) custom-call(bf16[2,256,512]{2,1,0:T(8,128)(2,1)S(1)} %get-tuple-element.4.solved, f32[2,256,512]{2,1,0:T(8,128)S(1)} %get-tuple-element.5.sigma), custom_call_target="tpu_custom_call" | custom-call | tf_op jit(solution)/shard_map/pallas_call | solution.py:513

commit v15 on v14

--- a/solution.py
+++ b/solution.py
@@ -233,13 +233,6 @@
     def settle(block, sem):
         pltpu.make_async_copy(block, block, sem).wait()
 
-    def others(body):
-        def one(step, carry):
-            body(lax.rem(me + step, n_mom))
-            return carry
-
-        return one
-
     def span(chunk):
         return pl.ds(pl.multiple_of(chunk * LANES, LANES), LANES)
 
@@ -285,10 +278,12 @@
             @pl.when(given)
             def _():
                 slot = slot_of(chunk)
-                lax.fori_loop(0, n_mom, others(lambda other: send(
-                    outbox.at[(chunk, other, *part)], inbox.at[(slot, me, *part)],
-                    in_send.at[chunk], in_recv.at[slot], other, core,
-                )), 0)
+                for step in range(n_mom):
+                    other = lax.rem(me + step, n_mom)
+                    send(
+                        outbox.at[(chunk, other, *part)], inbox.at[(slot, me, *part)],
+                        in_send.at[chunk], in_recv.at[slot], other, core,
+                    )
 
         spread((half,))
         return carry

time: 46.5 us -> 46.6 us (level)
  no operation moved by 1% of the time
where the time goes in v15:
time: 46.6 us; the launch traced here: 46.5 us
  Pallas kernels  45.8 us (98%)
  between operations  0.64 us (1%)
    pallas_call x1, Pallas kernels, local(): pl.pallas_call(kernel, out_shape=(pltpu.VMEM((2, rows, columns), bf16), p...  44.6 us
    pallas_call x1, Pallas kernels, local(): pl.pallas_call(write_out, out_shape=[jax.ShapeDtypeStruct(source.shape, d...  1.26 us

profile of v15, /device:TPU:24, one launch (start us, length us, event | category | flops | bytes accessed | tf_op | source)
XLA Modules:
  0.0 46.5 jit_solution(3000576361469083112)
XLA Ops:
  0.6 44.6 %shard_map.86 = (bf16[2,256,512]{2,1,0:T(8,128)(2,1)S(1)}, f32[2,256,512]{2,1,0:T(8,128)S(1)}) custom-call(s32[3,8,32]{2,1,0:T(8,128)} %bitcast.2, s32[32]{0:T(128)} %counts_hbm.1, s32[8,32]{1,0:T(8,128)} %bitcast.3, f32[16]{0:T(128)} %vertex_hbm.1, f32[2,1,256,512]{3,2,1,0:T(8,128)} %source_hbm.1, f32[2,1,1,256,256]{4,3,2,1,0:T(8,128)} %inverse_hbm.1, ...), custom_call_target="tpu_custom_call" | custom-call | tf_op jit(solution)/shard_map/pallas_call | solution.py:468
  45.2 1.3 %shard_map.87 = (bf16[2,1,256,512]{3,2,1,0:T(8,128)(2,1)}, f32[2,1,256,512]{3,2,1,0:T(8,128)}) custom-call(bf16[2,256,512]{2,1,0:T(8,128)(2,1)S(1)} %get-tuple-element.4.solved, f32[2,256,512]{2,1,0:T(8,128)S(1)} %get-tuple-element.5.sigma), custom_call_target="tpu_custom_call" | custom-call | tf_op jit(solution)/shard_map/pallas_call | solution.py:508
